TPU v7x, 128 devices: a whole 4x4x4 slice. The times are simulated.
128 devices in a mesh: ep: 32 (over z, y, core), rep: 4 (over x).
Axes of the slice: x: 4, y: 4, z: 4, core: 2. Of those that a mesh axis runs over, the one named last changes fastest.
Arguments:
- tokens: bfloat16 [16384, 2304], P(('ep', 'rep')), may hold values from -6 to 6
- output_grad: bfloat16 [16384, 2304], P(('ep', 'rep')), may hold values from -2 to 2
- chosen_experts: int32 [16384, 8], P(('ep', 'rep')), may hold values from 0 to 127, all different within a row; in each aligned block of 128 rows (0 to 127, 128 to 255, ...) at most 9 rows name the same one
- route_weights: float32 [16384, 8], P(('ep', 'rep')), may hold values from 0.1 to 0.5
- gate_weight: bfloat16 [128, 2304, 1024], P(('ep', 'rep')), may hold values from -0.125 to 0.125
- up_weight: bfloat16 [128, 2304, 1024], P(('ep', 'rep')), may hold values from -0.125 to 0.125
- down_weight: bfloat16 [128, 1024, 2304], P(('ep', 'rep')), may hold values from -0.1875 to 0.1875
- gate_adapter_in: bfloat16 [128, 16, 2304], P(('ep', 'rep')), may hold values from -0.125 to 0.125
- gate_adapter_out: bfloat16 [128, 16, 1024], P(('ep', 'rep')), may hold values from -1 to 1
- up_adapter_in: bfloat16 [128, 16, 2304], P(('ep', 'rep')), may hold values from -0.125 to 0.125
- up_adapter_out: bfloat16 [128, 16, 1024], P(('ep', 'rep')), may hold values from -1 to 1
- shared_gate: bfloat16 [2304, 512], P(None, 'rep'), may hold values from -0.125 to 0.125
- shared_up: bfloat16 [2304, 512], P(None, 'rep'), may hold values from -0.125 to 0.125
- shared_down: bfloat16 [2304, 512], P(None, 'rep'), may hold values from -0.25 to 0.25
Outputs:
- token_grad: bfloat16 [16384, 2304], P(('ep', 'rep'))
- gate_in_grad: float32 [128, 16, 2304], P(('ep', 'rep'))
- gate_out_grad: float32 [128, 16, 1024], P(('ep', 'rep'))
- up_in_grad: float32 [128, 16, 2304], P(('ep', 'rep'))
- up_out_grad: float32 [128, 16, 1024], P(('ep', 'rep'))
Inputs may be any that keep to these rules, and one draw needn't show every extreme that they name: `chosen_experts`: each row names 8 different experts. In each aligned block of 128 rows no expert is named by more than 9 rows, and in some block an expert is named by exactly 9 rows.
All inputs are finite; a program needn't handle non-finite values.
Results may differ from a plain program's by a relative error of at most 0.0064.
Values may be sent and summed in bfloat16 or wider, within the bound.
A program may use at most 128 MiB of HBM per device.

v0:
```python
import jax
import jax.numpy as jnp
from jax import lax
from jax.sharding import PartitionSpec as P


def contract_last(left, right):
    return lax.dot_general(
        left, right, (((1,), (1,)), ((), ())), preferred_element_type=jnp.float32
    )


def contract_first(left, right):
    return lax.dot_general(
        left, right, (((0,), (0,)), ((), ())), preferred_element_type=jnp.float32
    )


def expert_pass(input_rows, grad_rows, weights):
    gate_w, up_w, down_w, gate_in, gate_out, up_in, up_out = weights
    low_gate = contract_last(input_rows, gate_in).astype(jnp.bfloat16)
    low_up = contract_last(input_rows, up_in).astype(jnp.bfloat16)
    gate_pre = jnp.dot(input_rows, gate_w, preferred_element_type=jnp.float32) + jnp.dot(
        low_gate, gate_out, preferred_element_type=jnp.float32
    )
    up_pre = jnp.dot(input_rows, up_w, preferred_element_type=jnp.float32) + jnp.dot(
        low_up, up_out, preferred_element_type=jnp.float32
    )
    d_hidden = contract_last(grad_rows, down_w)
    gate_sigmoid = jax.nn.sigmoid(gate_pre)
    d_gate = (d_hidden * up_pre * gate_sigmoid * (1.0 + gate_pre * (1.0 - gate_sigmoid))).astype(
        jnp.bfloat16
    )
    d_up = (d_hidden * gate_pre * gate_sigmoid).astype(jnp.bfloat16)
    low_dgate = contract_last(d_gate, gate_out).astype(jnp.bfloat16)
    low_dup = contract_last(d_up, up_out).astype(jnp.bfloat16)
    row_grads = contract_last(d_gate, gate_w) + jnp.dot(
        low_dgate, gate_in, preferred_element_type=jnp.float32
    )
    row_grads = (
        row_grads
        + contract_last(d_up, up_w)
        + jnp.dot(low_dup, up_in, preferred_element_type=jnp.float32)
    )
    adapter_grads = (
        contract_first(low_dgate, input_rows),
        contract_first(low_gate, d_gate),
        contract_first(low_dup, input_rows),
        contract_first(low_up, d_up),
    )
    return (row_grads.astype(jnp.bfloat16), adapter_grads)


def shared_pass(input_rows, grad_rows, gate_w, up_w, down_w):
    gate_pre = jnp.dot(input_rows, gate_w, preferred_element_type=jnp.float32)
    up_pre = jnp.dot(input_rows, up_w, preferred_element_type=jnp.float32)
    d_hidden = jnp.dot(grad_rows, down_w, preferred_element_type=jnp.float32)
    gate_sigmoid = jax.nn.sigmoid(gate_pre)
    d_gate = (d_hidden * up_pre * gate_sigmoid * (1.0 + gate_pre * (1.0 - gate_sigmoid))).astype(
        jnp.bfloat16
    )
    d_up = (d_hidden * gate_pre * gate_sigmoid).astype(jnp.bfloat16)
    return contract_last(d_gate, gate_w) + contract_last(d_up, up_w)


def local(
    tokens,
    output_grad,
    chosen_experts,
    route_weights,
    gate_weight,
    up_weight,
    down_weight,
    gate_adapter_in,
    gate_adapter_out,
    up_adapter_in,
    up_adapter_out,
    shared_gate,
    shared_up,
    shared_down,
):
    ep_count = lax.axis_size("ep")
    rep_count = lax.axis_size("rep")
    owners = ep_count * rep_count
    token_rows, model_width = tokens.shape
    pick_count = chosen_experts.shape[1]
    pick_total = token_rows * pick_count
    slot_count = pick_total * 9 // (8 * owners)
    flat_experts = chosen_experts.reshape(pick_total)
    onehot = (flat_experts[:, None] == jnp.arange(owners, dtype=jnp.int32)[None, :]).astype(
        jnp.bfloat16
    )
    earlier = (jnp.arange(pick_total)[:, None] > jnp.arange(pick_total)[None, :]).astype(
        jnp.bfloat16
    )
    ahead_counts = jnp.dot(earlier, onehot, preferred_element_type=jnp.float32)
    position = jnp.sum(ahead_counts * onehot, axis=1).astype(jnp.int32)
    slot_index = flat_experts * slot_count + position
    scaled_grads = (
        (route_weights[:, :, None] * output_grad[:, None, :].astype(jnp.float32))
        .astype(jnp.bfloat16)
        .reshape(pick_total, model_width)
    )
    empty_slots = jnp.zeros((owners * slot_count, model_width), jnp.bfloat16)
    input_slots = (
        empty_slots.at[slot_index]
        .set(jnp.repeat(tokens, pick_count, axis=0))
        .reshape(owners, slot_count, model_width)
    )
    grad_slots = (
        empty_slots.at[slot_index].set(scaled_grads).reshape(owners, slot_count, model_width)
    )
    input_got, grad_got = (
        lax.all_to_all(input_slots, ("ep", "rep"), split_axis=0, concat_axis=0, tiled=True),
        lax.all_to_all(grad_slots, ("ep", "rep"), split_axis=0, concat_axis=0, tiled=True),
    )
    weights = (
        gate_weight[0],
        up_weight[0],
        down_weight[0],
        gate_adapter_in[0],
        gate_adapter_out[0],
        up_adapter_in[0],
        up_adapter_out[0],
    )
    row_grads, adapter_grads = expert_pass(
        input_got.reshape(owners * slot_count, model_width),
        grad_got.reshape(owners * slot_count, model_width),
        weights,
    )
    result_slots = row_grads.reshape(owners, slot_count, model_width)
    returned = lax.all_to_all(result_slots, ("ep", "rep"), split_axis=0, concat_axis=0, tiled=True)
    pick_grads = returned.reshape(owners * slot_count, model_width)[slot_index].reshape(
        token_rows, pick_count, model_width
    )
    routed_sum = jnp.sum(pick_grads.astype(jnp.float32), axis=1)
    every_tokens, every_grads = (
        lax.all_gather(tokens, "rep", axis=0, tiled=True),
        lax.all_gather(output_grad, "rep", axis=0, tiled=True),
    )
    shared_grad = lax.psum_scatter(
        shared_pass(every_tokens, every_grads, shared_gate, shared_up, shared_down),
        "rep",
        scatter_dimension=0,
        tiled=True,
    )
    token_grad = (routed_sum + shared_grad).astype(jnp.bfloat16)
    return (
        token_grad,
        adapter_grads[0][None],
        adapter_grads[1][None],
        adapter_grads[2][None],
        adapter_grads[3][None],
    )


def solution(mesh):
    in_specs = (
        P(("ep", "rep"), None),
        P(("ep", "rep"), None),
        P(("ep", "rep"), None),
        P(("ep", "rep"), None),
        P(("ep", "rep"), None, None),
        P(("ep", "rep"), None, None),
        P(("ep", "rep"), None, None),
        P(("ep", "rep"), None, None),
        P(("ep", "rep"), None, None),
        P(("ep", "rep"), None, None),
        P(("ep", "rep"), None, None),
        P(None, "rep"),
        P(None, "rep"),
        P(None, "rep"),
    )
    out_specs = (
        P(("ep", "rep"), None),
        P(("ep", "rep"), None, None),
        P(("ep", "rep"), None, None),
        P(("ep", "rep"), None, None),
        P(("ep", "rep"), None, None),
    )
    return jax.shard_map(local, mesh=mesh, in_specs=in_specs, out_specs=out_specs, check_vma=False)
```

profile of v0, /device:TPU:8, one launch (start us, length us, event | category | flops | bytes accessed | tf_op | source)
XLA Modules:
  0.0 550.6 jit_solution(18275145175907233703)
XLA Ops:
  10.3 10.6 %scatter_custom_fusion.1 = bf16[1152,2304]{1,0:T(8,128)(2,1)} fusion(s32[1024]{0:T(1024)S(1)} %bitcast.89, bf16[]{:T(256)} %constant.6.clone.1, bf16[128,2304]{1,0:T(8,128)(2,1)} %param.14), kind=kCustom, calls=%fused_computation.25 | custom fusion | bytes 5898242 | tf_op jit(solution)/shard_map/scatter | solution.py:107
  21.0 8.6 %reshape.78 = bf16[128,9,2304]{2,1,0:T(8,128)(2,1)} reshape(bf16[1152,2304]{1,0:T(8,128)(2,1)} %scatter_custom_fusion.1) | data formatting | bytes 10616832 | tf_op jit(solution)/shard_map/reshape | solution.py:108
  29.5 10.8 %all-to-all-start.1 = ((bf16[128,9,2304]{2,1,0:T(8,128)(2,1)}), bf16[128,9,2304]{2,1,0:T(8,128)(2,1)}, u32[]{:S(2)}, u32[]{:S(2)}) async-start(bf16[128,9,2304]{2,1,0:T(8,128)(2,1)} %reshape.78), calls=%async_computation.1 | async-start | bytes 18874368 | tf_op jit(solution)/shard_map/all_to_all | solution.py:114
  41.4 10.7 %scatter_custom_fusion = bf16[1152,2304]{1,0:T(8,128)(2,1)} fusion(s32[1024]{0:T(1024)S(1)} %bitcast.90, f32[128,2304]{1,0:T(8,128)S(1)} %convert_element_type.68, f32[1024]{0:T(1024)S(1)} %mul.77, bf16[]{:T(256)} %constant.6.clone.1), kind=kCustom, calls=%fused_computation.16 | custom fusion | flops 4718592 | bytes 6492162 | tf_op jit(solution)/shard_map/scatter | solution.py:111
  52.1 8.7 %reshape.75 = bf16[128,9,2304]{2,1,0:T(8,128)(2,1)} reshape(bf16[1152,2304]{1,0:T(8,128)(2,1)} %scatter_custom_fusion) | data formatting | bytes 10616832 | tf_op jit(solution)/shard_map/reshape | solution.py:111
  60.8 112.0 %all-to-all-done.1 = bf16[128,9,2304]{2,1,0:T(8,128)(2,1)} async-done(((bf16[128,9,2304]{2,1,0:T(8,128)(2,1)}), bf16[128,9,2304]{2,1,0:T(8,128)(2,1)}, u32[]{:S(2)}, u32[]{:S(2)}) %all-to-all-start.1) | async-done | bytes 5308448 | tf_op jit(solution)/shard_map/all_to_all | solution.py:114
  172.7 9.7 %all-to-all-start = ((bf16[128,9,2304]{2,1,0:T(8,128)(2,1)}), bf16[128,9,2304]{2,1,0:T(8,128)(2,1)}, u32[]{:S(2)}, u32[]{:S(2)}) async-start(bf16[128,9,2304]{2,1,0:T(8,128)(2,1)} %reshape.75), calls=%async_computation | async-start | bytes 18874368 | tf_op jit(solution)/shard_map/all_to_all | solution.py:115
  187.7 5.8 %fusion.32 = f32[512,2304]{1,0:T(8,128)} fusion(bf16[2304,128]{1,0:T(8,128)(2,1)} %param.25, f32[512,128]{1,0:T(8,128)S(1)} %fusion.50, bf16[512,2304]{1,0:T(8,128)(2,1)S(1)} %copy-done.3, bf16[2304,128]{1,0:T(8,128)(2,1)S(1)} %copy-done, f32[512,128]{1,0:T(8,128)S(1)} %fusion.51), kind=kOutput, calls=%fused_computation.52 | convolution fusion | flops 604635136 | bytes 8781824 | tf_op jit(solution)/shard_map/dot_general | solution.py:8
  193.5 5.3 convolution_add_fusion.2
  198.8 9.3 %reshape.79 = bf16[1152,2304]{1,0:T(8,128)(2,1)} reshape(bf16[128,9,2304]{2,1,0:T(8,128)(2,1)} %all-to-all-done.1) | data formatting | bytes 10616832 | tf_op jit(solution)/shard_map/reshape | solution.py:127
  214.7 8.5 %fusion.10 = f32[1152,1024]{1,0:T(8,128)S(1)} fusion(bf16[1152,2304]{1,0:T(8,128)(2,1)S(1)} %copy-done.2, bf16[1,2304,1024]{2,1,0:T(8,128)(2,1)} %param.18), kind=kOutput, calls=%fused_computation.19 | convolution fusion | flops 5435817984 | bytes 14745600 | tf_op jit(solution)/shard_map/dot_general | solution.py:23
  226.1 7.2 %fusion.14 = f32[1152,1024]{1,0:T(8,128)} fusion(bf16[1152,2304]{1,0:T(8,128)(2,1)S(1)} %copy-done.2, bf16[1,2304,1024]{2,1,0:T(8,128)(2,1)S(1)} %bitcast.94), kind=kOutput, calls=%fused_computation.23 | convolution fusion | flops 5435817984 | bytes 14745600 | tf_op jit(solution)/shard_map/dot_general | solution.py:26
  233.3 98.0 %all-to-all-done = bf16[128,9,2304]{2,1,0:T(8,128)(2,1)} async-done(((bf16[128,9,2304]{2,1,0:T(8,128)(2,1)}), bf16[128,9,2304]{2,1,0:T(8,128)(2,1)}, u32[]{:S(2)}, u32[]{:S(2)}) %all-to-all-start) | async-done | bytes 5308448 | tf_op jit(solution)/shard_map/all_to_all | solution.py:115
  331.3 9.1 %reshape.76 = bf16[1152,2304]{1,0:T(8,128)(2,1)} reshape(bf16[128,9,2304]{2,1,0:T(8,128)(2,1)} %all-to-all-done) | data formatting | bytes 10616832 | tf_op jit(solution)/shard_map/reshape | solution.py:128
  340.5 12.0 %multiply_convert_fusion = (bf16[1152,1024]{1,0:T(8,128)(2,1)S(1)}, f32[1152,1024]{1,0:T(8,128)S(1)}) fusion(f32[1152,1024]{1,0:T(8,128)} %convolution_add_fusion.3, bf16[1152,2304]{1,0:T(8,128)(2,1)} %reshape.76, bf16[1,1024,2304]{2,1,0:T(8,128)(2,1)} %param.20), kind=kOutput, calls=%fused_computation.29 | convolution fusion | flops 5442895872 | bytes 21823488 | tf_op jit(solution)/shard_map/dot_general | solution.py:8
  356.7 8.2 %fusion.8 = f32[1152,2304]{1,0:T(8,128)S(1)} fusion(bf16[1152,1024]{1,0:T(8,128)(2,1)S(1)} %fusion.23, bf16[1,2304,1024]{2,1,0:T(8,128)(2,1)} %param.18), kind=kOutput, calls=%fused_computation.17 | convolution fusion | flops 5435817984 | bytes 17694720 | tf_op jit(solution)/shard_map/dot_general | solution.py:8
  364.9 8.3 %fusion.12 = f32[1152,2304]{1,0:T(8,128)} fusion(bf16[1152,1024]{1,0:T(8,128)(2,1)S(1)} %get-tuple-element.5, bf16[1,2304,1024]{2,1,0:T(8,128)(2,1)S(1)} %bitcast.96), kind=kOutput, calls=%fused_computation.21 | convolution fusion | flops 5435817984 | bytes 17694720 | tf_op jit(solution)/shard_map/dot_general | solution.py:8
  373.2 5.9 %fusion = f32[1152,2304]{1,0:T(8,128)S(1)} fusion(f32[1152,2304]{1,0:T(8,128)} %fusion.12, f32[1152,2304]{1,0:T(8,128)S(1)} %fusion.8, bf16[1152,16]{0,1:T(8,128)(2,1)S(1)} %convolution_convert_fusion.1, bf16[1,16,2304]{2,1,0:T(8,128)(2,1)S(1)} %copy-done.8), kind=kOutput, calls=%fused_computation.5 | convolution fusion | flops 90243072 | bytes 31961088 | tf_op jit(solution)/shard_map/dot_general | solution.py:37
  383.0 8.5 %reshape.80 = bf16[128,9,2304]{2,1,0:T(8,128)(2,1)} reshape(bf16[1152,2304]{1,0:T(8,128)(2,1)} %fusion.1) | data formatting | bytes 10616832 | tf_op jit(solution)/shard_map/reshape | solution.py:131
  391.6 7.2 %all-to-all-start.2 = ((bf16[128,9,2304]{2,1,0:T(8,128)(2,1)}), bf16[128,9,2304]{2,1,0:T(8,128)(2,1)}, u32[]{:S(2)}, u32[]{:S(2)}) async-start(bf16[128,9,2304]{2,1,0:T(8,128)(2,1)} %reshape.80), calls=%async_computation.2 | async-start | bytes 18874368 | tf_op jit(solution)/shard_map/all_to_all | solution.py:132
  410.5 103.4 %all-to-all-done.2 = bf16[128,9,2304]{2,1,0:T(8,128)(2,1)} async-done(((bf16[128,9,2304]{2,1,0:T(8,128)(2,1)}), bf16[128,9,2304]{2,1,0:T(8,128)(2,1)}, u32[]{:S(2)}, u32[]{:S(2)}) %all-to-all-start.2) | async-done | bytes 5308448 | tf_op jit(solution)/shard_map/all_to_all | solution.py:132
  513.9 9.1 %reshape.81 = bf16[1152,2304]{1,0:T(8,128)(2,1)} reshape(bf16[128,9,2304]{2,1,0:T(8,128)(2,1)} %all-to-all-done.2) | data formatting | bytes 10616832 | tf_op jit(solution)/shard_map/reshape | solution.py:133
  523.0 13.0 %gather_fusion = bf16[1024,2304]{1,0:T(8,128)(2,1)} fusion(bf16[1152,2304]{1,0:T(8,128)(2,1)} %reshape.81, s32[1024]{0:T(1024)S(1)} %broadcast_clamp_fusion), kind=kCustom, calls=%fused_computation | custom fusion | bytes 9441280 | tf_op jit(solution)/shard_map/gather | solution.py:133
  536.0 5.4 convert_reduce_fusion
  (76 shorter events, 40.9 us)
Async XLA Ops:
  7.2 180.6 %copy-start = (bf16[2304,128]{1,0:T(8,128)(2,1)S(1)}, bf16[2304,128]{1,0:T(8,128)(2,1)}, u32[]{:S(2)}) copy-start(bf16[2304,128]{1,0:T(8,128)(2,1)} %param.26) | copy-start | bytes 1769476
  7.2 175.3 %all-gather.3.cloned.1.call-start = ((), (), s32[]{:S(2)}) async-start(), calls=%async_computation.4 | async-start | bytes 2949120 | tf_op jit(solution)/shard_map/all_gather | solution.py:139
  29.5 11.6 %copy-start.5 = (bf16[128,2304]{1,0:T(8,128)(2,1)S(1)}, bf16[128,2304]{1,0:T(8,128)(2,1)}, u32[]{:S(2)}) copy-start(bf16[128,2304]{1,0:T(8,128)(2,1)} %param.15) | copy-start | bytes 1769476
  29.5 11.7 %copy-start.11 = (f32[128,8]{0,1:T(8,128)S(1)}, f32[128,8]{0,1:T(8,128)}, u32[]{:S(2)}) copy-start(f32[128,8]{0,1:T(8,128)} %param.17) | copy-start | bytes 12292
  29.5 143.2 %all-to-all-start.1 = ((bf16[128,9,2304]{2,1,0:T(8,128)(2,1)}), bf16[128,9,2304]{2,1,0:T(8,128)(2,1)}, u32[]{:S(2)}, u32[]{:S(2)}) async-start(bf16[128,9,2304]{2,1,0:T(8,128)(2,1)} %reshape.78), calls=%async_computation.1 | async-start | bytes 18874368 | tf_op jit(solution)/shard_map/all_to_all | solution.py:114
  40.4 144.6 %all-gather.5.cloned.1.call-start = ((), (), s32[]{:S(2)}) async-start(), calls=%async_computation.5 | async-start | bytes 2949120 | tf_op jit(solution)/shard_map/all_gather | solution.py:138
  60.8 121.7 %copy-start.6 = (bf16[2304,128]{1,0:T(8,128)(2,1)S(1)}, bf16[2304,128]{1,0:T(8,128)(2,1)}, u32[]{:S(2)}) copy-start(bf16[2304,128]{1,0:T(8,128)(2,1)} %param.27) | copy-start | bytes 1769476
  172.7 158.6 %all-to-all-start = ((bf16[128,9,2304]{2,1,0:T(8,128)(2,1)}), bf16[128,9,2304]{2,1,0:T(8,128)(2,1)}, u32[]{:S(2)}, u32[]{:S(2)}) async-start(bf16[128,9,2304]{2,1,0:T(8,128)(2,1)} %reshape.75), calls=%async_computation | async-start | bytes 18874368 | tf_op jit(solution)/shard_map/all_to_all | solution.py:115
  182.5 359.0 %reduce-scatter.2.cloned.1.call-start = ((), (), s32[]{:S(2)}) async-start(), calls=%async_computation.6 | async-start | bytes 5898240 | tf_op jit(solution)/shard_map/reduce_scatter | solution.py:141
  198.8 9.3 %copy-start.8 = (bf16[1,16,2304]{2,1,0:T(8,128)(2,1)S(1)}, bf16[1,16,2304]{2,1,0:T(8,128)(2,1)}, u32[]{:S(2)}) copy-start(bf16[1,16,2304]{2,1,0:T(8,128)(2,1)} %param.21) | copy-start | bytes 221188
  208.1 5.0 copy-start.2
  208.1 5.0 copy-start.7
  213.2 12.9 %slice-start.2 = ((s8[4718592]{0:T(1024)(128)(4,1)}), s8[4194304]{0:T(1024)(128)(4,1)S(1)}, s32[]{:S(2)}) async-start(s8[4718592]{0:T(1024)(128)(4,1)} %bitcast.93), calls=%async_computation.9 | async-start | bytes 8388608
  214.7 8.5 %copy-start.9 = (bf16[1,16,1024]{2,1,0:T(8,128)(2,1)S(1)}, bf16[1,16,1024]{2,1,0:T(8,128)(2,1)}, u32[]{:S(2)}) copy-start(bf16[1,16,1024]{2,1,0:T(8,128)(2,1)} %param.22) | copy-start | bytes 98308
  214.7 11.4 %slice-start.3 = ((s8[4718592]{0:T(1024)(128)(4,1)}), s8[524288]{0:T(1024)(128)(4,1)S(1)}, s32[]{:S(2)}) async-start(s8[4718592]{0:T(1024)(128)(4,1)} %bitcast.93), calls=%async_computation.10 | async-start | bytes 1048576
  331.3 21.9 %slice-start = ((s8[4718592]{0:T(1024)(128)(4,1)}), s8[524288]{0:T(1024)(128)(4,1)S(1)}, s32[]{:S(2)}) async-start(s8[4718592]{0:T(1024)(128)(4,1)} %bitcast.87), calls=%async_computation.7 | async-start | bytes 1048576
  340.5 12.0 %copy-start.10 = (bf16[1,16,1024]{2,1,0:T(8,128)(2,1)S(1)}, bf16[1,16,1024]{2,1,0:T(8,128)(2,1)}, u32[]{:S(2)}) copy-start(bf16[1,16,1024]{2,1,0:T(8,128)(2,1)} %param.24) | copy-start | bytes 98308
  340.5 12.7 %slice-start.1 = ((s8[4718592]{0:T(1024)(128)(4,1)}), s8[4194304]{0:T(1024)(128)(4,1)S(1)}, s32[]{:S(2)}) async-start(s8[4718592]{0:T(1024)(128)(4,1)} %bitcast.87), calls=%async_computation.8 | async-start | bytes 8388608
  340.5 12.8 %copy-start.12 = (f32[1152,1024]{1,0:T(8,128)S(1)}, f32[1152,1024]{1,0:T(8,128)}, u32[]{:S(2)}) copy-start(f32[1152,1024]{1,0:T(8,128)} %fusion.14) | copy-start | bytes 14155780
  353.2 11.6 %slice-start.4 = ((s8[4718592]{0:T(1024)(128)(4,1)}), s8[4194304]{0:T(1024)(128)(4,1)S(1)}, s32[]{:S(2)}) async-start(s8[4718592]{0:T(1024)(128)(4,1)} %bitcast.95), calls=%async_computation.11 | async-start | bytes 8388608
  356.0 8.9 %copy-start.4 = (bf16[1152,1024]{1,0:T(8,128)(2,1)}, bf16[1152,1024]{1,0:T(8,128)(2,1)S(1)}, u32[]{:S(2)}) copy-start(bf16[1152,1024]{1,0:T(8,128)(2,1)S(1)} %fusion.23) | copy-start | bytes 7077892
  356.7 8.2 %slice-start.5 = ((s8[4718592]{0:T(1024)(128)(4,1)}), s8[524288]{0:T(1024)(128)(4,1)S(1)}, s32[]{:S(2)}) async-start(s8[4718592]{0:T(1024)(128)(4,1)} %bitcast.95), calls=%async_computation.12 | async-start | bytes 1048576
  391.6 122.3 %all-to-all-start.2 = ((bf16[128,9,2304]{2,1,0:T(8,128)(2,1)}), bf16[128,9,2304]{2,1,0:T(8,128)(2,1)}, u32[]{:S(2)}, u32[]{:S(2)}) async-start(bf16[128,9,2304]{2,1,0:T(8,128)(2,1)} %reshape.80), calls=%async_computation.2 | async-start | bytes 18874368 | tf_op jit(solution)/shard_map/all_to_all | solution.py:132
  523.0 20.7 %copy-start.1 = (bf16[2304,128]{1,0:T(8,128)(2,1)S(1)}, bf16[2304,128]{1,0:T(8,128)(2,1)}, u32[]{:S(2)}) copy-start(bf16[2304,128]{1,0:T(8,128)(2,1)} %param.26) | copy-start | bytes 1769476
  (1 other events, 2.7 us)
Sparse Core Ops, SparseCore 0:
  9.7 36.9 all-gather.2
  48.3 70.2 all-gather.4
  199.0 123.8 reduce-scatter.1
where the time goes:
time: 560 us; the launch traced here: 551 us
  waiting for transfers between devices  314 us (56%)
  matrix products  96 us (17%)
  local copies, waits for them, and re-layouts  78.3 us (14%)
  starting transfers between devices  28.3 us (5%)
  other arithmetic  19.1 us (3%)
  between operations  14.5 us (3%)
    all_to_all x1, waiting for transfers between devices, local(): lax.all_to_all(input_slots, ('ep', 'rep'), split_axis=0, concat_axis=0, t...  112 us
    all_to_all x1, waiting for transfers between devices, local(): lax.all_to_all(result_slots, ('ep', 'rep'), split_axis=0, concat_axis=0,...  103 us
    all_to_all x1, waiting for transfers between devices, local(): lax.all_to_all(grad_slots, ('ep', 'rep'), split_axis=0, concat_axis=0, ti...  98 us
    dot_general x9, matrix products, contract_last(): lax.dot_general(left, right, (((1,), (1,)), ((), ())), preferred_element_...  47.4 us
    gather x1, local copies, waits for them, and re-layouts, local(): returned.reshape(owners * slot_count, model_width)[slot_index]  13 us
    dot_general x4, matrix products, contract_first(): lax.dot_general(left, right, (((0,), (0,)), ((), ())), preferred_element_...  11.7 us
  transfers between devices with their start and end apart: 6, of which 3 were waited for; matrix products, arithmetic and copies ran while one was open for 35% of the time, Pallas kernels for 0%

commit v1 on v0

v1 whole, which is shorter than its diff:
```python
import functools

import jax
import jax.numpy as jnp
import numpy as np
from jax import lax
from jax.experimental import pallas as pl
from jax.experimental.pallas import tpu as pltpu
from jax.sharding import PartitionSpec as P

MESH = pl.DeviceIdType.MESH
BF = jnp.bfloat16
F32 = jnp.float32

TD = 128
D = 2304
FF = 1024
CAP = 9
NB = 8
NPEER = 16
MSG = NB * CAP
ROWS = NPEER * MSG
GR = 4 * MSG
ND = 3
CW = D // ND
NP = 2 * ND
HALF = 4 * TD


def dot(a, b):
    return jnp.dot(a, b, preferred_element_type=F32)


def dot_last(a, b):
    return lax.dot_general(a, b, (((1,), (1,)), ((), ())), preferred_element_type=F32)


def dot_first(a, b):
    return lax.dot_general(a, b, (((0,), (0,)), ((), ())), preferred_element_type=F32)


def position():
    e, x = lax.axis_index("ep"), lax.axis_index("rep")
    return e // 8, (e // 2) % 4, e % 2, x


def peer(i, sign):
    z, y, c, x = position()
    oy = i % 4
    oz = (i % 4 + i // 4) % 4
    zz = (z + sign * oz + 4) % 4
    yy = (y + sign * oy + 4) % 4
    return {"ep": (zz * 4 + yy) * 2 + c, "rep": x}


def x_peer(o):
    z, y, c, x = position()
    return {"ep": (z * 4 + y) * 2 + c, "rep": (x + o) % 4}


def member(o):
    z, y, c, x = position()
    return {"ep": (z * 4 + y) * 2 + (c + o // 4) % 2, "rep": (x + o) % 4}


def member_slot(o):
    z, y, c, x = position()
    return ((c + o // 4) % 2) * 4 + (x + o) % 4


def sibling():
    z, y, c, x = position()
    return {"ep": (z * 4 + y) * 2 + 1 - c, "rep": x}


def remote(src, dst, send, recv, device):
    return pltpu.make_async_remote_copy(
        src_ref=src,
        dst_ref=dst,
        send_sem=send,
        recv_sem=recv,
        device_id=device,
        device_id_type=MESH,
    )


def wait_for(ref, sem):
    pltpu.make_async_copy(ref, ref, sem).wait()


def kernel(
    tok,
    grd,
    meta,
    expand,
    slot_of,
    block_of,
    block_row,
    gw_h,
    uw_h,
    dw_h,
    gin,
    gout,
    uin,
    uout,
    sg_h,
    su_h,
    sd_h,
    out,
    gin_g,
    gout_g,
    uin_g,
    uout_g,
    sb,
    rb,
    ob,
    ret,
    gw,
    uw,
    dw,
    sg,
    su,
    sd,
    meta_all,
    xg,
    place,
    place_t,
    wsl,
    tmp,
    stage,
    xb,
    gb,
    dg,
    du,
    outb,
    sga,
    sua,
    sda,
    sdg,
    sdu,
    retv,
    own,
    csb,
    crb,
    xsb,
    xrb,
    fin,
    w_sem,
    s_sem,
    m_send,
    m_recv,
    m_own,
    own_sem,
    gx_send,
    gx_recv,
    gc_send,
    gc_recv,
    st_sem,
    d_send,
    d_recv,
    d_own,
    in_sem,
    o_sem,
    r_send,
    r_recv,
    r_own,
    rv_sem,
    c_send,
    c_recv,
    x_send,
    x_recv,
    f_sem,
):
    z, y, c, x = position()
    me = c * 4 + x

    barrier = pltpu.get_barrier_semaphore()

    @pl.loop(1, NPEER)
    def _(i):
        pl.semaphore_signal(barrier, inc=1, device_id=peer(i, 1), device_id_type=MESH)

    @pl.loop(1, 8)
    def _(o):
        pl.semaphore_signal(barrier, inc=1, device_id=member(o), device_id_type=MESH)

    weights = [(gw_h, gw), (uw_h, uw), (dw_h, dw)]
    shared = [(sg_h, sg), (su_h, su), (sd_h, sd)]
    own_meta = pltpu.make_async_copy(meta.at[me], meta_all.at[me], m_own)
    own_meta.start()

    def own_piece(p):
        src = tok if p < ND else grd
        return pltpu.make_async_copy(
            src.at[:, pl.ds((p % ND) * CW, CW)],
            xg.at[p, pl.ds(me * TD, TD), :],
            own_sem.at[p],
        )

    for p in range(NP):
        own_piece(p).start()
    for h, v in shared:
        pltpu.make_async_copy(h, v, s_sem).start()
    for j, (h, v) in enumerate(weights):
        pltpu.make_async_copy(h, v, w_sem.at[j]).start()
    gin_g[...] = jnp.zeros_like(gin_g)
    gout_g[...] = jnp.zeros_like(gout_g)
    uin_g[...] = jnp.zeros_like(uin_g)
    uout_g[...] = jnp.zeros_like(uout_g)
    sga[...] = jnp.zeros_like(sga)
    sua[...] = jnp.zeros_like(sua)
    sda[...] = jnp.zeros_like(sda)

    pl.semaphore_wait(barrier, NPEER - 1 + 7)

    @pl.loop(1, 8)
    def _(o):
        remote(meta.at[member_slot(o)], meta_all.at[me], m_send, m_recv, member(o)).start()

    for p in range(NP):
        src = (tok if p < ND else grd).at[:, pl.ds((p % ND) * CW, CW)]
        dst = xg.at[p, pl.ds(me * TD, TD), :]
        for o in (1, 3, 2):
            remote(src, dst, gx_send, gx_recv.at[p, o - 1], x_peer(o)).start()
        remote(src, dst, gc_send, gc_recv.at[p], sibling()).start()

    own_meta.wait()
    wait_for(meta_all.at[pl.ds(0, 7)], m_recv)

    spread = expand[...]
    code = meta_all[:, 0].reshape(TD, TD).astype(BF)
    hit = jnp.where(dot(spread, code) == slot_of[...], 1.0, 0.0)
    w_all = meta_all[:, 1].reshape(TD, TD)
    w_hi = w_all.astype(BF)
    left = w_all - w_hi.astype(F32)
    w_mid = left.astype(BF)
    w_lo = (left - w_mid.astype(F32)).astype(BF)
    w_row = (dot(spread, w_hi) + dot(spread, w_mid)) + dot(spread, w_lo)
    wsl[...] = jnp.broadcast_to(jnp.sum(w_row * hit, axis=1, keepdims=True), (ROWS, TD))
    hit_t = hit.T
    for b in range(NB):
        place[:, b * TD : (b + 1) * TD] = jnp.where(block_of[...] == float(b), hit, 0.0).astype(BF)
        place_t[b * TD : (b + 1) * TD, :] = (hit_t * block_row[b : b + 1, :]).astype(BF)

    wait_shared = [pltpu.make_async_copy(h, v, s_sem) for h, v in shared]
    for cp in wait_shared:
        cp.wait()

    mine = pl.multiple_of(c * HALF, HALF)
    other = pl.multiple_of((1 - c) * HALF, HALF)

    def rows_of(k):
        return pl.ds(pl.multiple_of(k * GR, 8), GR)

    def send_piece(p, k, slot):
        cp = pltpu.make_async_copy(stage.at[slot], sb.at[p, rows_of(k), :], st_sem)
        cp.start()
        cp.wait()

        @pl.loop(0, 4)
        def _(j):
            i = k * 4 + j
            rows = pl.ds(pl.multiple_of(i * MSG, 8), MSG)

            @pl.when(i > 0)
            def _():
                remote(
                    sb.at[p, rows, :], rb.at[p, rows, :], d_send, d_recv.at[k], peer(i, 1)
                ).start()

            @pl.when(i == 0)
            def _():
                pltpu.make_async_copy(sb.at[p, rows, :], rb.at[p, rows, :], d_own).start()

    def scaled(acc, p, k):
        scale = jnp.where(p < ND, 1.0, wsl[rows_of(k), :][:, 0:1])
        return (acc * scale).astype(BF)

    def arrive(p):
        for o in (1, 3, 2):
            slot = pl.ds(pl.multiple_of((c * 4 + (x + 4 - o) % 4) * TD, TD), TD)
            block = xg.at[p, slot, :]
            wait_for(block, gx_recv.at[p, o - 1])
            remote(block, block, gc_send, gc_recv.at[p], sibling()).start()

    def first_groups(p, shared_part):
        arrive(p)

        @pl.loop(0, 2)
        def _(k):
            for n in range(3):
                cols = slice(n * 256, (n + 1) * 256)
                tmp[k, :, cols] = dot(
                    place[rows_of(k), pl.ds(mine, HALF)], xg[p, pl.ds(mine, HALF), cols]
                )

        wait_for(xg.at[p, pl.ds(other, HALF), :], gc_recv.at[p])

        @pl.loop(0, 2)
        def _(k):
            for n in range(3):
                cols = slice(n * 256, (n + 1) * 256)
                acc = tmp[k, :, cols] + dot(
                    place[rows_of(k), pl.ds(other, HALF)], xg[p, pl.ds(other, HALF), cols]
                )
                stage[k, :, cols] = scaled(acc, p, k)
            send_piece(p, k, k)

        shared_part(xg[p, pl.ds(mine, HALF), :])

    @pl.loop(0, ND)
    def _(d):
        pltpu.make_async_copy(
            tok.at[:, pl.ds(0, CW)], xg.at[d, pl.ds(me * TD, TD), :], own_sem.at[d]
        ).wait()
        rows = pl.ds(pl.multiple_of(d * CW, CW), CW)

        def part(block):
            sga[...] += dot(block, sg[rows, :])
            sua[...] += dot(block, su[rows, :])

        first_groups(d, part)

    @pl.loop(0, ND)
    def _(d):
        p = d + ND
        pltpu.make_async_copy(
            tok.at[:, pl.ds(0, CW)], xg.at[p, pl.ds(me * TD, TD), :], own_sem.at[p]
        ).wait()
        rows = pl.ds(pl.multiple_of(d * CW, CW), CW)

        def part(block):
            sda[...] += dot(block, sd[rows, :])

        first_groups(p, part)

    s_gate, s_up, s_hid = sga[...], sua[...], sda[...]
    sig = jax.nn.sigmoid(s_gate)
    sdg[...] = (s_hid * s_up * sig * (1.0 + s_gate * (1.0 - sig))).astype(BF)
    sdu[...] = (s_hid * s_gate * sig).astype(BF)

    for j, (h, v) in enumerate(weights):
        pltpu.make_async_copy(h, v, w_sem.at[j]).wait()

    def late_group(k):
        @pl.loop(0, NP)
        def _(p):
            for n in range(3):
                cols = slice(n * 256, (n + 1) * 256)
                acc = dot(place[rows_of(k), :], xg[p, :, cols])
                stage[0, :, cols] = scaled(acc, p, k)
            send_piece(p, k, 0)

    def fetch(k):
        for d in range(ND):
            pltpu.make_async_copy(rb.at[d, rows_of(k), :], xb.at[d], in_sem).start()
            pltpu.make_async_copy(rb.at[ND + d, rows_of(k), :], gb.at[d], in_sem).start()
        wait_for(xb, in_sem)
        wait_for(gb, in_sem)

    def expert(k):
        low_gate = sum(dot_last(xb[d], gin[:, d * CW : (d + 1) * CW]) for d in range(ND)).astype(BF)
        low_up = sum(dot_last(xb[d], uin[:, d * CW : (d + 1) * CW]) for d in range(ND)).astype(BF)

        @pl.loop(0, FF // 256)
        def _(j):
            cols = pl.ds(pl.multiple_of(j * 256, 256), 256)
            gate = sum(dot(xb[d], gw[d * CW : (d + 1) * CW, cols]) for d in range(ND))
            gate = gate + dot(low_gate, gout[:, cols])
            up = sum(dot(xb[d], uw[d * CW : (d + 1) * CW, cols]) for d in range(ND))
            up = up + dot(low_up, uout[:, cols])
            hid = sum(dot_last(gb[d], dw[cols, d * CW : (d + 1) * CW]) for d in range(ND))
            s = jax.nn.sigmoid(gate)
            dg[:, cols] = (hid * up * s * (1.0 + gate * (1.0 - s))).astype(BF)
            du[:, cols] = (hid * gate * s).astype(BF)

        dgv, duv = dg[...], du[...]
        low_dg = dot_last(dgv, gout[...]).astype(BF)
        low_du = dot_last(duv, uout[...]).astype(BF)
        gout_g[...] += dot_first(low_gate, dgv)
        uout_g[...] += dot_first(low_up, duv)
        for d in range(ND):
            cols = slice(d * CW, (d + 1) * CW)
            gin_g[:, cols] += dot_first(low_dg, xb[d])
            uin_g[:, cols] += dot_first(low_du, xb[d])

        @pl.loop(0, ND)
        def _(d):
            for n in range(3):
                rows = pl.ds(pl.multiple_of(d * CW + n * 256, 256), 256)
                acc = dot_last(dg[...], gw[rows, :]) + dot(low_dg, gin[:, rows])
                acc = acc + dot_last(du[...], uw[rows, :]) + dot(low_du, uin[:, rows])
                outb[d, :, n * 256 : (n + 1) * 256] = acc.astype(BF)

    def send_back(k):
        for d in range(ND):
            pltpu.make_async_copy(outb.at[d], ob.at[d, rows_of(k), :], o_sem).start()
        wait_for(outb, o_sem)

        @pl.loop(0, ND)
        def _(d):
            @pl.loop(0, 4)
            def _(j):
                i = k * 4 + j
                rows = pl.ds(pl.multiple_of(i * MSG, 8), MSG)

                @pl.when(i > 0)
                def _():
                    remote(
                        ob.at[d, rows, :], ret.at[d, rows, :], r_send, r_recv.at[d], peer(i, -1)
                    ).start()

                @pl.when(i == 0)
                def _():
                    pltpu.make_async_copy(ob.at[d, rows, :], ret.at[d, rows, :], r_own).start()

    @pl.loop(0, 4)
    def _(k):
        @pl.when(k < 2)
        def _():
            late_group(k + 2)

        @pl.when(k == 0)
        def _():
            wait_for(rb.at[:, pl.ds(0, 3 * MSG), :], d_recv.at[0])
            wait_for(rb.at[:, pl.ds(0, MSG), :], d_own)

        @pl.when(k > 0)
        def _():
            wait_for(rb.at[:, pl.ds(0, GR), :], d_recv.at[k])

        fetch(k)
        expert(k)
        send_back(k)

    wait_for(ret.at[:, pl.ds(0, MSG), :], r_own)

    @pl.loop(0, ND + 1)
    def _(t):
        @pl.when(t < ND)
        def _():
            d = jnp.minimum(t, ND - 1)
            wait_for(ret.at[d, pl.ds(0, ROWS - MSG), :], r_recv.at[d])
            cp = pltpu.make_async_copy(ret.at[d], retv, rv_sem)
            cp.start()
            cp.wait()
            for m in range(2):
                for n in range(3):
                    cols = slice(n * 256, (n + 1) * 256)
                    rows = pl.ds(pl.multiple_of(other + m * 256, 256), 256)
                    csb[d, m * 256 : (m + 1) * 256, cols] = dot(
                        place_t[rows, :], retv[:, cols]
                    ).astype(BF)
            remote(csb.at[d], crb.at[d], c_send, c_recv.at[d], sibling()).start()
            for m in range(2):
                for n in range(3):
                    cols = slice(n * 256, (n + 1) * 256)
                    here = slice(m * 256, (m + 1) * 256)
                    rows = pl.ds(pl.multiple_of(mine + m * 256, 256), 256)
                    wide = pl.ds(pl.multiple_of(d * CW + n * 256, 256), 256)
                    acc = dot(place_t[rows, :], retv[:, cols])
                    acc = acc + dot_last(sdg[here, :], sg[wide, :])
                    own[d, here, cols] = acc + dot_last(sdu[here, :], su[wide, :])

        @pl.when(t > 0)
        def _():
            d = jnp.maximum(t - 1, 0)
            wait_for(crb.at[d], c_recv.at[d])
            own[d] = own[d] + crb[d].astype(F32)
            for o in (2, 1, 3):
                slot = pl.ds(pl.multiple_of(((x + o) % 4) * TD, TD), TD)
                xsb[d, o - 1] = own[d, slot, :].astype(BF)
                remote(
                    xsb.at[d, o - 1], xrb.at[d, o - 1], x_send, x_recv.at[d], x_peer(o)
                ).start()

    @pl.loop(0, ND)
    def _(d):
        wait_for(xrb.at[d], x_recv.at[d])
        total = own[d, pl.ds(pl.multiple_of(x * TD, TD), TD), :]
        for o in range(3):
            total = total + xrb[d, o].astype(F32)
        fin[d] = total.astype(BF)

    for d in range(ND):
        pltpu.make_async_copy(fin.at[d], out.at[:, pl.ds(d * CW, CW)], f_sem).start()

    wait_for(meta_all.at[pl.ds(0, 7)], m_send)
    wait_for(xg.at[:, pl.ds(0, 3 * TD), :], gx_send)
    wait_for(xg.at[:, pl.ds(0, 4 * TD), :], gc_send)
    wait_for(sb.at[:, pl.ds(0, ROWS - MSG), :], d_send)
    wait_for(ob.at[:, pl.ds(0, ROWS - MSG), :], r_send)
    wait_for(csb, c_send)
    wait_for(xsb, x_send)
    wait_for(fin, f_sem)


def tables():
    r = np.arange(ROWS)
    i, b, s = r // MSG, (r // CAP) % NB, r % CAP
    expand = (np.arange(TD)[None, :] == (b * NPEER + i)[:, None]).astype(np.float32)
    slot_of = np.broadcast_to(s[:, None], (ROWS, TD)).astype(np.float32)
    block_of = np.broadcast_to(b[:, None], (ROWS, TD)).astype(np.float32)
    block_row = (b[None, :] == np.arange(NB)[:, None]).astype(np.float32)
    return expand, slot_of, block_of, block_row


def local(
    tokens,
    output_grad,
    chosen_experts,
    route_weights,
    gate_weight,
    up_weight,
    down_weight,
    gate_adapter_in,
    gate_adapter_out,
    up_adapter_in,
    up_adapter_out,
    shared_gate,
    shared_up,
    shared_down,
):
    z, y, c, x = position()
    g = jnp.arange(NB)[:, None]
    i = jnp.arange(NPEER)[None, :]
    zz = (z + i % 4 + i // 4) % 4
    yy = (y + i % 4) % 4
    ids = (((zz * 4 + yy) * 2 + g // 4) * 4 + g % 4).reshape(TD)
    same = chosen_experts.T[None, :, :] == ids[:, None, None]
    picked = jnp.any(same, axis=1)
    slot_weight = jnp.sum(jnp.where(same, route_weights.T[None, :, :], 0.0), axis=1)
    before = (jnp.arange(TD)[:, None] < jnp.arange(TD)[None, :]).astype(BF)
    place = jnp.dot(picked.astype(BF), before, preferred_element_type=F32)
    code = jnp.where(picked, place, -1.0)
    meta = jnp.stack(
        [code.reshape(NB, NPEER, TD), slot_weight.reshape(NB, NPEER, TD)], axis=1
    )
    expand, slot_of, block_of, block_row = tables()
    any_spec = pl.BlockSpec(memory_space=pl.ANY)
    vmem = pl.BlockSpec(memory_space=pltpu.VMEM)
    rank = gate_adapter_in.shape[1]
    sff = shared_gate.shape[1]
    dma = pltpu.SemaphoreType.DMA
    shape = jax.ShapeDtypeStruct
    outs = pl.pallas_call(
        kernel,
        name="moe_backward",
        out_shape=(
            shape((TD, D), BF),
            shape((rank, D), F32),
            shape((rank, FF), F32),
            shape((rank, D), F32),
            shape((rank, FF), F32),
            shape((NP, ROWS, CW), BF),
            shape((NP, ROWS, CW), BF),
            shape((ND, ROWS, CW), BF),
            shape((ND, ROWS, CW), BF),
        ),
        in_specs=[any_spec] * 3
        + [vmem] * 4
        + [any_spec] * 3
        + [vmem] * 4
        + [any_spec] * 3,
        out_specs=(any_spec, vmem, vmem, vmem, vmem) + (any_spec,) * 4,
        scratch_shapes=[
            pltpu.VMEM((D, FF), BF),
            pltpu.VMEM((D, FF), BF),
            pltpu.VMEM((FF, D), BF),
            pltpu.VMEM((D, sff), BF),
            pltpu.VMEM((D, sff), BF),
            pltpu.VMEM((D, sff), BF),
            pltpu.VMEM((NB, 2, NPEER, TD), F32),
            pltpu.VMEM((NP, NB * TD, CW), BF),
            pltpu.VMEM((ROWS, NB * TD), BF),
            pltpu.VMEM((NB * TD, ROWS), BF),
            pltpu.VMEM((ROWS, TD), F32),
            pltpu.VMEM((2, GR, CW), F32),
            pltpu.VMEM((2, GR, CW), BF),
            pltpu.VMEM((ND, GR, CW), BF),
            pltpu.VMEM((ND, GR, CW), BF),
            pltpu.VMEM((GR, FF), BF),
            pltpu.VMEM((GR, FF), BF),
            pltpu.VMEM((ND, GR, CW), BF),
            pltpu.VMEM((HALF, sff), F32),
            pltpu.VMEM((HALF, sff), F32),
            pltpu.VMEM((HALF, sff), F32),
            pltpu.VMEM((HALF, sff), BF),
            pltpu.VMEM((HALF, sff), BF),
            pltpu.VMEM((ROWS, CW), BF),
            pltpu.VMEM((ND, HALF, CW), F32),
            pltpu.VMEM((ND, HALF, CW), BF),
            pltpu.VMEM((ND, HALF, CW), BF),
            pltpu.VMEM((ND, 3, TD, CW), BF),
            pltpu.VMEM((ND, 3, TD, CW), BF),
            pltpu.VMEM((ND, TD, CW), BF),
            dma((3,)),
            dma,
            dma,
            dma,
            dma,
            dma((NP,)),
            dma,
            dma((NP, 3)),
            dma,
            dma((NP,)),
            dma,
            dma,
            dma((4,)),
            dma,
            dma,
            dma,
            dma,
            dma((ND,)),
            dma,
            dma,
            dma,
            dma((ND,)),
            dma,
            dma((ND,)),
            dma,
        ],
        compiler_params=pltpu.CompilerParams(
            collective_id=0, has_side_effects=True, vmem_limit_bytes=62 << 20
        ),
    )(
        tokens,
        output_grad,
        meta,
        jnp.asarray(expand, BF),
        jnp.asarray(slot_of),
        jnp.asarray(block_of),
        jnp.asarray(block_row),
        gate_weight[0],
        up_weight[0],
        down_weight[0],
        gate_adapter_in[0],
        gate_adapter_out[0],
        up_adapter_in[0],
        up_adapter_out[0],
        shared_gate,
        shared_up,
        shared_down,
    )
    return (outs[0], outs[1][None], outs[2][None], outs[3][None], outs[4][None])


def solution(mesh):
    in_specs = (
        (P(("ep", "rep"), None),) * 4 + (P(("ep", "rep"), None, None),) * 7 + (P(None, "rep"),) * 3
    )
    out_specs = (P(("ep", "rep"), None),) + (P(("ep", "rep"), None, None),) * 4
    return jax.shard_map(
        local, mesh=mesh, in_specs=in_specs, out_specs=out_specs, check_vma=False
    )
```

time: 560 us -> 291 us (0.52)
  the two profiles are of different devices: /device:TPU:8 before, /device:TPU:60 now
where the time goes in v1:
time: 291 us; the launch traced here: 290 us
  Pallas kernels  279 us (96%)
  local copies, waits for them, and re-layouts  8.1 us (3%)
    pallas_call x1, Pallas kernels, local(): pl.pallas_call(kernel, name='moe_backward', out_shape=(shape((TD, D), BF)...  279 us
    unnamed x5, local copies, waits for them, and re-layouts  8.02 us

profile of v1, /device:TPU:60, one launch (start us, length us, event | category | flops | bytes accessed | tf_op | source)
XLA Modules:
  0.0 290.2 jit_solution(12619664072830390067)
XLA Ops:
  0.7 0.1 multiply_add_fusion
  0.8 0.1 add.149
  0.9 0.9 compare_reduce_fusion
  1.8 0.1 convolution_select_fusion
  1.9 0.9 fusion
  2.9 0.7 pad_maximum_fusion.meta
  3.5 278.6 %moe_backward.1 = (bf16[128,2304]{1,0:T(8,128)(2,1)}, f32[16,2304]{1,0:T(8,128)}, f32[16,1024]{1,0:T(8,128)}, f32[16,2304]{1,0:T(8,128)}, f32[16,1024]{1,0:T(8,1...) custom-call(bf16[128,2304]{1,0:T(8,128)(2,1)} %tok.1, ...), custom_call_target="tpu_custom_call" | custom-call | tf_op jit(solution)/shard_map/moe_backward/pallas_call | solution.py:546
  282.1 1.9 copy.28
  284.1 1.6 copy.29
  285.6 1.5 copy.30
  287.1 1.6 copy.31
  288.7 1.5 copy.32
  (2 shorter events, 0.0 us)

commit v2 on v1

--- a/solution.py
+++ b/solution.py
@@ -91,7 +91,8 @@
 def kernel(
     tok,
     grd,
-    meta,
+    chosen,
+    route,
     expand,
     slot_of,
     block_of,
@@ -121,6 +122,7 @@
     sg,
     su,
     sd,
+    meta,
     meta_all,
     xg,
     place,
@@ -133,6 +135,7 @@
     dg,
     du,
     outb,
+    kept,
     sga,
     sua,
     sda,
@@ -186,8 +189,6 @@
 
     weights = [(gw_h, gw), (uw_h, uw), (dw_h, dw)]
     shared = [(sg_h, sg), (su_h, su), (sd_h, sd)]
-    own_meta = pltpu.make_async_copy(meta.at[me], meta_all.at[me], m_own)
-    own_meta.start()
 
     def own_piece(p):
         src = tok if p < ND else grd
@@ -210,6 +211,25 @@
     sga[...] = jnp.zeros_like(sga)
     sua[...] = jnp.zeros_like(sua)
     sda[...] = jnp.zeros_like(sda)
+
+    row_i = lax.broadcasted_iota(jnp.int32, (TD, TD), 0)
+    col_i = lax.broadcasted_iota(jnp.int32, (TD, TD), 1)
+    group, chip = row_i >> 4, row_i & 15
+    zz = (z + (chip & 3) + (chip >> 2)) & 3
+    yy = (y + (chip & 3)) & 3
+    ids = (((zz * 4 + yy) * 2 + (group >> 2)) * 4) + (group & 3)
+    picked = jnp.zeros((TD, TD), F32)
+    weight = jnp.zeros((TD, TD), F32)
+    for k in range(chosen.shape[0]):
+        same = chosen[k : k + 1, :] == ids
+        picked = jnp.where(same, 1.0, picked)
+        weight = jnp.where(same, route[k : k + 1, :], weight)
+    before = jnp.where(row_i < col_i, 1.0, 0.0).astype(BF)
+    count = dot(picked.astype(BF), before)
+    meta[:, 0] = jnp.where(picked > 0.0, count, -1.0).reshape(NB, NPEER, TD)
+    meta[:, 1] = weight.reshape(NB, NPEER, TD)
+    own_meta = pltpu.make_async_copy(meta.at[me], meta_all.at[me], m_own)
+    own_meta.start()
 
     pl.semaphore_wait(barrier, NPEER - 1 + 7)
 
@@ -270,7 +290,8 @@
 
             @pl.when(i == 0)
             def _():
-                pltpu.make_async_copy(sb.at[p, rows, :], rb.at[p, rows, :], d_own).start()
+                kept[p] = stage[slot, 0:MSG, :]
+                pltpu.make_async_copy(kept.at[p], rb.at[p, rows, :], d_own).start()
 
     def scaled(acc, p, k):
         scale = jnp.where(p < ND, 1.0, wsl[rows_of(k), :][:, 0:1])
@@ -342,14 +363,12 @@
     for j, (h, v) in enumerate(weights):
         pltpu.make_async_copy(h, v, w_sem.at[j]).wait()
 
-    def late_group(k):
-        @pl.loop(0, NP)
-        def _(p):
-            for n in range(3):
-                cols = slice(n * 256, (n + 1) * 256)
-                acc = dot(place[rows_of(k), :], xg[p, :, cols])
-                stage[0, :, cols] = scaled(acc, p, k)
-            send_piece(p, k, 0)
+    def late_piece(k, p):
+        for n in range(3):
+            cols = slice(n * 256, (n + 1) * 256)
+            acc = dot(place[rows_of(k), :], xg[p, :, cols])
+            stage[0, :, cols] = scaled(acc, p, k)
+        send_piece(p, k, 0)
 
     def fetch(k):
         for d in range(ND):
@@ -392,16 +411,22 @@
                 acc = acc + dot_last(du[...], uw[rows, :]) + dot(low_du, uin[:, rows])
                 outb[d, :, n * 256 : (n + 1) * 256] = acc.astype(BF)
 
-    def send_back(k):
+    def store(k):
         for d in range(ND):
             pltpu.make_async_copy(outb.at[d], ob.at[d, rows_of(k), :], o_sem).start()
         wait_for(outb, o_sem)
 
-        @pl.loop(0, ND)
+        @pl.when(k == 0)
+        def _():
+            for d in range(ND):
+                kept[d] = outb[d, 0:MSG, :]
+                pltpu.make_async_copy(kept.at[d], ret.at[d, pl.ds(0, MSG), :], r_own).start()
+
+    def send_back(k_from, k_to, d_from, d_to):
+        @pl.loop(d_from, d_to)
         def _(d):
-            @pl.loop(0, 4)
-            def _(j):
-                i = k * 4 + j
+            @pl.loop(4 * k_from, 4 * k_to)
+            def _(i):
                 rows = pl.ds(pl.multiple_of(i * MSG, 8), MSG)
 
                 @pl.when(i > 0)
@@ -410,16 +435,15 @@
                         ob.at[d, rows, :], ret.at[d, rows, :], r_send, r_recv.at[d], peer(i, -1)
                     ).start()
 
-                @pl.when(i == 0)
-                def _():
-                    pltpu.make_async_copy(ob.at[d, rows, :], ret.at[d, rows, :], r_own).start()
+
+    @pl.loop(2, 4)
+    def _(k):
+        @pl.loop(0, NP)
+        def _(p):
+            late_piece(k, p)
 
     @pl.loop(0, 4)
     def _(k):
-        @pl.when(k < 2)
-        def _():
-            late_group(k + 2)
-
         @pl.when(k == 0)
         def _():
             wait_for(rb.at[:, pl.ds(0, 3 * MSG), :], d_recv.at[0])
@@ -431,7 +455,20 @@
 
         fetch(k)
         expert(k)
-        send_back(k)
+        store(k)
+
+        @pl.when(k < 3)
+        def _():
+            send_back(k, k + 1, 0, 1)
+
+        @pl.when(k == 2)
+        def _():
+            send_back(0, 3, 1, 2)
+
+        @pl.when(k == 3)
+        def _():
+            send_back(3, 4, 0, 2)
+            send_back(0, 4, 2, 3)
 
     wait_for(ret.at[:, pl.ds(0, MSG), :], r_own)
 
@@ -495,6 +532,11 @@
     wait_for(fin, f_sem)
 
 
+def hand_over(*refs):
+    for j in range(5):
+        refs[5 + j][...] = refs[j][...].reshape(refs[5 + j].shape)
+
+
 def tables():
     r = np.arange(ROWS)
     i, b, s = r // MSG, (r // CAP) % NB, r % CAP
@@ -521,21 +563,6 @@
     shared_up,
     shared_down,
 ):
-    z, y, c, x = position()
-    g = jnp.arange(NB)[:, None]
-    i = jnp.arange(NPEER)[None, :]
-    zz = (z + i % 4 + i // 4) % 4
-    yy = (y + i % 4) % 4
-    ids = (((zz * 4 + yy) * 2 + g // 4) * 4 + g % 4).reshape(TD)
-    same = chosen_experts.T[None, :, :] == ids[:, None, None]
-    picked = jnp.any(same, axis=1)
-    slot_weight = jnp.sum(jnp.where(same, route_weights.T[None, :, :], 0.0), axis=1)
-    before = (jnp.arange(TD)[:, None] < jnp.arange(TD)[None, :]).astype(BF)
-    place = jnp.dot(picked.astype(BF), before, preferred_element_type=F32)
-    code = jnp.where(picked, place, -1.0)
-    meta = jnp.stack(
-        [code.reshape(NB, NPEER, TD), slot_weight.reshape(NB, NPEER, TD)], axis=1
-    )
     expand, slot_of, block_of, block_row = tables()
     any_spec = pl.BlockSpec(memory_space=pl.ANY)
     vmem = pl.BlockSpec(memory_space=pltpu.VMEM)
@@ -557,8 +584,8 @@
             shape((ND, ROWS, CW), BF),
             shape((ND, ROWS, CW), BF),
         ),
-        in_specs=[any_spec] * 3
-        + [vmem] * 4
+        in_specs=[any_spec] * 2
+        + [vmem] * 6
         + [any_spec] * 3
         + [vmem] * 4
         + [any_spec] * 3,
@@ -571,6 +598,7 @@
             pltpu.VMEM((D, sff), BF),
             pltpu.VMEM((D, sff), BF),
             pltpu.VMEM((NB, 2, NPEER, TD), F32),
+            pltpu.VMEM((NB, 2, NPEER, TD), F32),
             pltpu.VMEM((NP, NB * TD, CW), BF),
             pltpu.VMEM((ROWS, NB * TD), BF),
             pltpu.VMEM((NB * TD, ROWS), BF),
@@ -582,6 +610,7 @@
             pltpu.VMEM((GR, FF), BF),
             pltpu.VMEM((GR, FF), BF),
             pltpu.VMEM((ND, GR, CW), BF),
+            pltpu.VMEM((NP, MSG, CW), BF),
             pltpu.VMEM((HALF, sff), F32),
             pltpu.VMEM((HALF, sff), F32),
             pltpu.VMEM((HALF, sff), F32),
@@ -626,7 +655,8 @@
     )(
         tokens,
         output_grad,
-        meta,
+        chosen_experts.T,
+        route_weights.T,
         jnp.asarray(expand, BF),
         jnp.asarray(slot_of),
         jnp.asarray(block_of),
@@ -642,7 +672,19 @@
         shared_up,
         shared_down,
     )
-    return (outs[0], outs[1][None], outs[2][None], outs[3][None], outs[4][None])
+    return pl.pallas_call(
+        hand_over,
+        name="hand_over",
+        out_shape=(
+            shape((TD, D), BF),
+            shape((1, rank, D), F32),
+            shape((1, rank, FF), F32),
+            shape((1, rank, D), F32),
+            shape((1, rank, FF), F32),
+        ),
+        in_specs=[vmem] * 5,
+        out_specs=(vmem,) * 5,
+    )(*outs[:5])
 
 
 def solution(mesh):

time: 291 us -> 260 us (0.89)
  the two profiles are of different devices: /device:TPU:60 before, /device:TPU:8 now
where the time goes in v2:
time: 260 us; the launch traced here: 256 us
  Pallas kernels  255 us (98%)
    pallas_call x1, Pallas kernels, local(): pl.pallas_call(kernel, name='moe_backward', out_shape=(shape((TD, D), BF)...  253 us

profile of v2, /device:TPU:8, one launch (start us, length us, event | category | flops | bytes accessed | tf_op | source)
XLA Modules:
  0.0 256.1 jit_solution(1002059623651863300)
XLA Ops:
  0.6 253.3 %moe_backward.1 = (bf16[128,2304]{1,0:T(8,128)(2,1)}, f32[16,2304]{1,0:T(8,128)}, f32[16,1024]{1,0:T(8,128)}, f32[16,2304]{1,0:T(8,128)}, f32[16,1024]{1,0:T(8,1...) custom-call(bf16[128,2304]{1,0:T(8,128)(2,1)} %tok.1, ...), custom_call_target="tpu_custom_call" | custom-call | tf_op jit(solution)/shard_map/moe_backward/pallas_call | solution.py:573
  253.9 2.2 hand_over.1

commit v3 on v2

--- a/solution.py
+++ b/solution.py
@@ -25,6 +25,9 @@
 CW = D // ND
 NP = 2 * ND
 HALF = 4 * TD
+UW = 256
+NU = D // UW
+FIRST = 3
 
 
 def dot(a, b):
@@ -128,6 +131,7 @@
     place,
     place_t,
     wsl,
+    hits,
     tmp,
     stage,
     xb,
@@ -136,6 +140,7 @@
     du,
     outb,
     kept,
+    back,
     sga,
     sua,
     sda,
@@ -257,10 +262,9 @@
     w_lo = (left - w_mid.astype(F32)).astype(BF)
     w_row = (dot(spread, w_hi) + dot(spread, w_mid)) + dot(spread, w_lo)
     wsl[...] = jnp.broadcast_to(jnp.sum(w_row * hit, axis=1, keepdims=True), (ROWS, TD))
-    hit_t = hit.T
+    hits[...] = hit
     for b in range(NB):
         place[:, b * TD : (b + 1) * TD] = jnp.where(block_of[...] == float(b), hit, 0.0).astype(BF)
-        place_t[b * TD : (b + 1) * TD, :] = (hit_t * block_row[b : b + 1, :]).astype(BF)
 
     wait_shared = [pltpu.make_async_copy(h, v, s_sem) for h, v in shared]
     for cp in wait_shared:
@@ -307,7 +311,7 @@
     def first_groups(p, shared_part):
         arrive(p)
 
-        @pl.loop(0, 2)
+        @pl.loop(0, FIRST)
         def _(k):
             for n in range(3):
                 cols = slice(n * 256, (n + 1) * 256)
@@ -317,7 +321,7 @@
 
         wait_for(xg.at[p, pl.ds(other, HALF), :], gc_recv.at[p])
 
-        @pl.loop(0, 2)
+        @pl.loop(0, FIRST)
         def _(k):
             for n in range(3):
                 cols = slice(n * 256, (n + 1) * 256)
@@ -409,22 +413,23 @@
                 rows = pl.ds(pl.multiple_of(d * CW + n * 256, 256), 256)
                 acc = dot_last(dg[...], gw[rows, :]) + dot(low_dg, gin[:, rows])
                 acc = acc + dot_last(du[...], uw[rows, :]) + dot(low_du, uin[:, rows])
-                outb[d, :, n * 256 : (n + 1) * 256] = acc.astype(BF)
+                outb[3 * d + n] = acc.astype(BF)
 
     def store(k):
-        for d in range(ND):
-            pltpu.make_async_copy(outb.at[d], ob.at[d, rows_of(k), :], o_sem).start()
+        @pl.loop(0, NU)
+        def _(u):
+            pltpu.make_async_copy(outb.at[u], ob.at[u, rows_of(k), :], o_sem).start()
+
         wait_for(outb, o_sem)
 
         @pl.when(k == 0)
         def _():
-            for d in range(ND):
-                kept[d] = outb[d, 0:MSG, :]
-                pltpu.make_async_copy(kept.at[d], ret.at[d, pl.ds(0, MSG), :], r_own).start()
-
-    def send_back(k_from, k_to, d_from, d_to):
-        @pl.loop(d_from, d_to)
-        def _(d):
+            back[...] = outb[:, 0:MSG, :]
+            pltpu.make_async_copy(back, ret.at[:, pl.ds(0, MSG), :], r_own).start()
+
+    def send_back(k_from, k_to, u_from, u_to):
+        @pl.loop(u_from, u_to)
+        def _(u):
             @pl.loop(4 * k_from, 4 * k_to)
             def _(i):
                 rows = pl.ds(pl.multiple_of(i * MSG, 8), MSG)
@@ -432,16 +437,19 @@
                 @pl.when(i > 0)
                 def _():
                     remote(
-                        ob.at[d, rows, :], ret.at[d, rows, :], r_send, r_recv.at[d], peer(i, -1)
+                        ob.at[u, rows, :], ret.at[u, rows, :], r_send, r_recv.at[u], peer(i, -1)
                     ).start()
 
-
-    @pl.loop(2, 4)
+    @pl.loop(FIRST, 4)
     def _(k):
         @pl.loop(0, NP)
         def _(p):
             late_piece(k, p)
 
+    hit_t = hits[...].T
+    for b in range(NB):
+        place_t[b * TD : (b + 1) * TD, :] = (hit_t * block_row[b : b + 1, :]).astype(BF)
+
     @pl.loop(0, 4)
     def _(k):
         @pl.when(k == 0)
@@ -459,68 +467,60 @@
 
         @pl.when(k < 3)
         def _():
-            send_back(k, k + 1, 0, 1)
+            send_back(k, k + 1, 0, 3)
 
         @pl.when(k == 2)
         def _():
-            send_back(0, 3, 1, 2)
+            send_back(0, 3, 3, 6)
 
         @pl.when(k == 3)
         def _():
-            send_back(3, 4, 0, 2)
-            send_back(0, 4, 2, 3)
+            send_back(3, 4, 0, 6)
+            send_back(0, 4, 6, NU)
 
     wait_for(ret.at[:, pl.ds(0, MSG), :], r_own)
 
-    @pl.loop(0, ND + 1)
+    def combine(u):
+        wide = pl.ds(pl.multiple_of(u * UW, UW), UW)
+        wait_for(ret.at[u, pl.ds(0, ROWS - MSG), :], r_recv.at[u])
+        cp = pltpu.make_async_copy(ret.at[u], retv, rv_sem)
+        cp.start()
+        cp.wait()
+        csb[u] = dot(place_t[pl.ds(other, HALF), :], retv[...]).astype(BF)
+        remote(csb.at[u], crb.at[u], c_send, c_recv.at[u], sibling()).start()
+        acc = dot(place_t[pl.ds(mine, HALF), :], retv[...])
+        own[u] = acc + (dot_last(sdg[...], sg[wide, :]) + dot_last(sdu[...], su[wide, :]))
+
+    def across(u):
+        wait_for(crb.at[u], c_recv.at[u])
+        own[u] = own[u] + crb[u].astype(F32)
+        for o in (2, 1, 3):
+            slot = pl.ds(pl.multiple_of(((x + o) % 4) * TD, TD), TD)
+            xsb[u, o - 1] = own[u, slot, :].astype(BF)
+            remote(xsb.at[u, o - 1], xrb.at[u, o - 1], x_send, x_recv.at[u], x_peer(o)).start()
+
+    def finish(u):
+        wait_for(xrb.at[u], x_recv.at[u])
+        total = own[u, pl.ds(pl.multiple_of(x * TD, TD), TD), :]
+        for o in range(3):
+            total = total + xrb[u, o].astype(F32)
+        fin[u] = total.astype(BF)
+        wide = pl.ds(pl.multiple_of(u * UW, UW), UW)
+        pltpu.make_async_copy(fin.at[u], out.at[:, wide], f_sem).start()
+
+    @pl.loop(0, NU + 2)
     def _(t):
-        @pl.when(t < ND)
-        def _():
-            d = jnp.minimum(t, ND - 1)
-            wait_for(ret.at[d, pl.ds(0, ROWS - MSG), :], r_recv.at[d])
-            cp = pltpu.make_async_copy(ret.at[d], retv, rv_sem)
-            cp.start()
-            cp.wait()
-            for m in range(2):
-                for n in range(3):
-                    cols = slice(n * 256, (n + 1) * 256)
-                    rows = pl.ds(pl.multiple_of(other + m * 256, 256), 256)
-                    csb[d, m * 256 : (m + 1) * 256, cols] = dot(
-                        place_t[rows, :], retv[:, cols]
-                    ).astype(BF)
-            remote(csb.at[d], crb.at[d], c_send, c_recv.at[d], sibling()).start()
-            for m in range(2):
-                for n in range(3):
-                    cols = slice(n * 256, (n + 1) * 256)
-                    here = slice(m * 256, (m + 1) * 256)
-                    rows = pl.ds(pl.multiple_of(mine + m * 256, 256), 256)
-                    wide = pl.ds(pl.multiple_of(d * CW + n * 256, 256), 256)
-                    acc = dot(place_t[rows, :], retv[:, cols])
-                    acc = acc + dot_last(sdg[here, :], sg[wide, :])
-                    own[d, here, cols] = acc + dot_last(sdu[here, :], su[wide, :])
-
-        @pl.when(t > 0)
-        def _():
-            d = jnp.maximum(t - 1, 0)
-            wait_for(crb.at[d], c_recv.at[d])
-            own[d] = own[d] + crb[d].astype(F32)
-            for o in (2, 1, 3):
-                slot = pl.ds(pl.multiple_of(((x + o) % 4) * TD, TD), TD)
-                xsb[d, o - 1] = own[d, slot, :].astype(BF)
-                remote(
-                    xsb.at[d, o - 1], xrb.at[d, o - 1], x_send, x_recv.at[d], x_peer(o)
-                ).start()
-
-    @pl.loop(0, ND)
-    def _(d):
-        wait_for(xrb.at[d], x_recv.at[d])
-        total = own[d, pl.ds(pl.multiple_of(x * TD, TD), TD), :]
-        for o in range(3):
-            total = total + xrb[d, o].astype(F32)
-        fin[d] = total.astype(BF)
-
-    for d in range(ND):
-        pltpu.make_async_copy(fin.at[d], out.at[:, pl.ds(d * CW, CW)], f_sem).start()
+        @pl.when(t < NU)
+        def _():
+            combine(jnp.minimum(t, NU - 1))
+
+        @pl.when((t > 0) & (t <= NU))
+        def _():
+            across(jnp.clip(t - 1, 0, NU - 1))
+
+        @pl.when(t > 1)
+        def _():
+            finish(jnp.maximum(t - 2, 0))
 
     wait_for(meta_all.at[pl.ds(0, 7)], m_send)
     wait_for(xg.at[:, pl.ds(0, 3 * TD), :], gx_send)
@@ -581,8 +581,8 @@
             shape((rank, FF), F32),
             shape((NP, ROWS, CW), BF),
             shape((NP, ROWS, CW), BF),
-            shape((ND, ROWS, CW), BF),
-            shape((ND, ROWS, CW), BF),
+            shape((NU, ROWS, UW), BF),
+            shape((NU, ROWS, UW), BF),
         ),
         in_specs=[any_spec] * 2
         + [vmem] * 6
@@ -603,26 +603,28 @@
             pltpu.VMEM((ROWS, NB * TD), BF),
             pltpu.VMEM((NB * TD, ROWS), BF),
             pltpu.VMEM((ROWS, TD), F32),
-            pltpu.VMEM((2, GR, CW), F32),
-            pltpu.VMEM((2, GR, CW), BF),
+            pltpu.VMEM((ROWS, TD), F32),
+            pltpu.VMEM((FIRST, GR, CW), F32),
+            pltpu.VMEM((FIRST, GR, CW), BF),
             pltpu.VMEM((ND, GR, CW), BF),
             pltpu.VMEM((ND, GR, CW), BF),
             pltpu.VMEM((GR, FF), BF),
             pltpu.VMEM((GR, FF), BF),
-            pltpu.VMEM((ND, GR, CW), BF),
+            pltpu.VMEM((NU, GR, UW), BF),
             pltpu.VMEM((NP, MSG, CW), BF),
+            pltpu.VMEM((NU, MSG, UW), BF),
             pltpu.VMEM((HALF, sff), F32),
             pltpu.VMEM((HALF, sff), F32),
             pltpu.VMEM((HALF, sff), F32),
             pltpu.VMEM((HALF, sff), BF),
             pltpu.VMEM((HALF, sff), BF),
-            pltpu.VMEM((ROWS, CW), BF),
-            pltpu.VMEM((ND, HALF, CW), F32),
-            pltpu.VMEM((ND, HALF, CW), BF),
-            pltpu.VMEM((ND, HALF, CW), BF),
-            pltpu.VMEM((ND, 3, TD, CW), BF),
-            pltpu.VMEM((ND, 3, TD, CW), BF),
-            pltpu.VMEM((ND, TD, CW), BF),
+            pltpu.VMEM((ROWS, UW), BF),
+            pltpu.VMEM((NU, HALF, UW), F32),
+            pltpu.VMEM((NU, HALF, UW), BF),
+            pltpu.VMEM((NU, HALF, UW), BF),
+            pltpu.VMEM((NU, 3, TD, UW), BF),
+            pltpu.VMEM((NU, 3, TD, UW), BF),
+            pltpu.VMEM((NU, TD, UW), BF),
             dma((3,)),
             dma,
             dma,
@@ -640,13 +642,13 @@
             dma,
             dma,
             dma,
-            dma((ND,)),
-            dma,
-            dma,
-            dma,
-            dma((ND,)),
-            dma,
-            dma((ND,)),
+            dma((NU,)),
+            dma,
+            dma,
+            dma,
+            dma((NU,)),
+            dma,
+            dma((NU,)),
             dma,
         ],
         compiler_params=pltpu.CompilerParams(

time: 260 us -> 237 us (0.912)
  the two profiles are of different devices: /device:TPU:8 before, /device:TPU:16 now
where the time goes in v3:
time: 237 us
  Pallas kernels  236 us (100%)
    pallas_call x1, Pallas kernels, local(): pl.pallas_call(kernel, name='moe_backward', out_shape=(shape((TD, D), BF)...  234 us

profile of v3, /device:TPU:16, one launch (start us, length us, event | category | flops | bytes accessed | tf_op | source)
XLA Modules:
  0.0 236.6 jit_solution(7552672689481270747)
XLA Ops:
  0.6 233.8 %moe_backward.1 = (bf16[128,2304]{1,0:T(8,128)(2,1)}, f32[16,2304]{1,0:T(8,128)}, f32[16,1024]{1,0:T(8,128)}, f32[16,2304]{1,0:T(8,128)}, f32[16,1024]{1,0:T(8,1...) custom-call(bf16[128,2304]{1,0:T(8,128)(2,1)} %tok.1, ...), custom_call_target="tpu_custom_call" | custom-call | tf_op jit(solution)/shard_map/moe_backward/pallas_call | solution.py:573
  234.4 2.2 hand_over.1

commit v4 on v3

--- a/solution.py
+++ b/solution.py
@@ -1,8 +1,5 @@
-import functools
-
 import jax
 import jax.numpy as jnp
-import numpy as np
 from jax import lax
 from jax.experimental import pallas as pl
 from jax.experimental.pallas import tpu as pltpu
@@ -23,7 +20,8 @@
 GR = 4 * MSG
 ND = 3
 CW = D // ND
-NP = 2 * ND
+NA = 2
+PIECES = ((0, 0, 1), (0, 1, 2), (0, 3, 3), (0, 6, 3), (1, 0, 3), (1, 3, 3), (1, 6, 3))
 HALF = 4 * TD
 UW = 256
 NU = D // UW
@@ -51,8 +49,9 @@
     z, y, c, x = position()
     oy = i % 4
     oz = (i % 4 + i // 4) % 4
-    zz = (z + sign * oz + 4) % 4
-    yy = (y + sign * oy + 4) % 4
+    way = sign * (1 - 2 * c)
+    zz = (z + way * oz + 4) % 4
+    yy = (y + way * oy + 4) % 4
     return {"ep": (zz * 4 + yy) * 2 + c, "rep": x}
 
 
@@ -96,10 +95,6 @@
     grd,
     chosen,
     route,
-    expand,
-    slot_of,
-    block_of,
-    block_row,
     gw_h,
     uw_h,
     dw_h,
@@ -195,16 +190,14 @@
     weights = [(gw_h, gw), (uw_h, uw), (dw_h, dw)]
     shared = [(sg_h, sg), (su_h, su), (sd_h, sd)]
 
-    def own_piece(p):
-        src = tok if p < ND else grd
-        return pltpu.make_async_copy(
-            src.at[:, pl.ds((p % ND) * CW, CW)],
-            xg.at[p, pl.ds(me * TD, TD), :],
-            own_sem.at[p],
-        )
-
-    for p in range(NP):
-        own_piece(p).start()
+    def piece_of(p):
+        a, first, width = PIECES[p]
+        cols = pl.ds(first * UW, width * UW)
+        return (grd if a else tok).at[:, cols], xg.at[a, pl.ds(me * TD, TD), cols]
+
+    for p in range(len(PIECES)):
+        src, dst = piece_of(p)
+        pltpu.make_async_copy(src, dst, own_sem.at[p]).start()
     for h, v in shared:
         pltpu.make_async_copy(h, v, s_sem).start()
     for j, (h, v) in enumerate(weights):
@@ -220,8 +213,9 @@
     row_i = lax.broadcasted_iota(jnp.int32, (TD, TD), 0)
     col_i = lax.broadcasted_iota(jnp.int32, (TD, TD), 1)
     group, chip = row_i >> 4, row_i & 15
-    zz = (z + (chip & 3) + (chip >> 2)) & 3
-    yy = (y + (chip & 3)) & 3
+    way = 1 - 2 * (group >> 2)
+    zz = (z + way * ((chip & 3) + (chip >> 2)) + 8) & 3
+    yy = (y + way * (chip & 3) + 8) & 3
     ids = (((zz * 4 + yy) * 2 + (group >> 2)) * 4) + (group & 3)
     picked = jnp.zeros((TD, TD), F32)
     weight = jnp.zeros((TD, TD), F32)
@@ -242,19 +236,24 @@
     def _(o):
         remote(meta.at[member_slot(o)], meta_all.at[me], m_send, m_recv, member(o)).start()
 
-    for p in range(NP):
-        src = (tok if p < ND else grd).at[:, pl.ds((p % ND) * CW, CW)]
-        dst = xg.at[p, pl.ds(me * TD, TD), :]
+    for p in range(len(PIECES)):
+        src, dst = piece_of(p)
         for o in (1, 3, 2):
             remote(src, dst, gx_send, gx_recv.at[p, o - 1], x_peer(o)).start()
         remote(src, dst, gc_send, gc_recv.at[p], sibling()).start()
 
+    row = lax.broadcasted_iota(jnp.int32, (ROWS, TD), 0)
+    lane = lax.broadcasted_iota(jnp.int32, (ROWS, TD), 1)
+    nine = (row * 7282) >> 16
+    slot_of = (row - CAP * nine).astype(F32)
+    block_of = nine & 7
+    spread = jnp.where(lane == block_of * NPEER + (nine >> 3), 1.0, 0.0).astype(BF)
+
     own_meta.wait()
     wait_for(meta_all.at[pl.ds(0, 7)], m_recv)
 
-    spread = expand[...]
     code = meta_all[:, 0].reshape(TD, TD).astype(BF)
-    hit = jnp.where(dot(spread, code) == slot_of[...], 1.0, 0.0)
+    hit = jnp.where(dot(spread, code) == slot_of, 1.0, 0.0)
     w_all = meta_all[:, 1].reshape(TD, TD)
     w_hi = w_all.astype(BF)
     left = w_all - w_hi.astype(F32)
@@ -264,7 +263,7 @@
     wsl[...] = jnp.broadcast_to(jnp.sum(w_row * hit, axis=1, keepdims=True), (ROWS, TD))
     hits[...] = hit
     for b in range(NB):
-        place[:, b * TD : (b + 1) * TD] = jnp.where(block_of[...] == float(b), hit, 0.0).astype(BF)
+        place[:, b * TD : (b + 1) * TD] = jnp.where(block_of == b, hit, 0.0).astype(BF)
 
     wait_shared = [pltpu.make_async_copy(h, v, s_sem) for h, v in shared]
     for cp in wait_shared:
@@ -276,8 +275,9 @@
     def rows_of(k):
         return pl.ds(pl.multiple_of(k * GR, 8), GR)
 
-    def send_piece(p, k, slot):
-        cp = pltpu.make_async_copy(stage.at[slot], sb.at[p, rows_of(k), :], st_sem)
+    def send_piece(a, cols, width, k, slot):
+        filled = stage.at[slot, :, pl.ds(0, width)]
+        cp = pltpu.make_async_copy(filled, sb.at[a, rows_of(k), cols], st_sem)
         cp.start()
         cp.wait()
 
@@ -289,75 +289,70 @@
             @pl.when(i > 0)
             def _():
                 remote(
-                    sb.at[p, rows, :], rb.at[p, rows, :], d_send, d_recv.at[k], peer(i, 1)
+                    sb.at[a, rows, cols], rb.at[a, rows, cols], d_send, d_recv.at[k], peer(i, 1)
                 ).start()
 
             @pl.when(i == 0)
             def _():
-                kept[p] = stage[slot, 0:MSG, :]
-                pltpu.make_async_copy(kept.at[p], rb.at[p, rows, :], d_own).start()
-
-    def scaled(acc, p, k):
-        scale = jnp.where(p < ND, 1.0, wsl[rows_of(k), :][:, 0:1])
+                kept[a, :, cols] = stage[slot, 0:MSG, 0:width]
+                pltpu.make_async_copy(kept.at[a, :, cols], rb.at[a, rows, cols], d_own).start()
+
+    def scaled(acc, a, k):
+        scale = jnp.where(a == 0, 1.0, wsl[rows_of(k), :][:, 0:1])
         return (acc * scale).astype(BF)
 
-    def arrive(p):
+    def units(first, n):
+        return pl.ds(pl.multiple_of((first + n) * UW, UW), UW)
+
+    def first_groups(p, a, first, count):
+        width = count * UW
+        cols = pl.ds(pl.multiple_of(first * UW, UW), width)
+        own_block = xg.at[a, pl.ds(me * TD, TD), cols]
+        wait_for(own_block, own_sem.at[p])
         for o in (1, 3, 2):
             slot = pl.ds(pl.multiple_of((c * 4 + (x + 4 - o) % 4) * TD, TD), TD)
-            block = xg.at[p, slot, :]
+            block = xg.at[a, slot, cols]
             wait_for(block, gx_recv.at[p, o - 1])
             remote(block, block, gc_send, gc_recv.at[p], sibling()).start()
 
-    def first_groups(p, shared_part):
-        arrive(p)
-
         @pl.loop(0, FIRST)
         def _(k):
-            for n in range(3):
-                cols = slice(n * 256, (n + 1) * 256)
-                tmp[k, :, cols] = dot(
-                    place[rows_of(k), pl.ds(mine, HALF)], xg[p, pl.ds(mine, HALF), cols]
+            for n in range(count):
+                tmp[k, :, n * UW : (n + 1) * UW] = dot(
+                    place[rows_of(k), pl.ds(mine, HALF)], xg[a, pl.ds(mine, HALF), units(first, n)]
                 )
 
-        wait_for(xg.at[p, pl.ds(other, HALF), :], gc_recv.at[p])
+        wait_for(xg.at[a, pl.ds(other, HALF), cols], gc_recv.at[p])
 
         @pl.loop(0, FIRST)
         def _(k):
-            for n in range(3):
-                cols = slice(n * 256, (n + 1) * 256)
-                acc = tmp[k, :, cols] + dot(
-                    place[rows_of(k), pl.ds(other, HALF)], xg[p, pl.ds(other, HALF), cols]
+            for n in range(count):
+                here = slice(n * UW, (n + 1) * UW)
+                acc = tmp[k, :, here] + dot(
+                    place[rows_of(k), pl.ds(other, HALF)],
+                    xg[a, pl.ds(other, HALF), units(first, n)],
                 )
-                stage[k, :, cols] = scaled(acc, p, k)
-            send_piece(p, k, k)
-
-        shared_part(xg[p, pl.ds(mine, HALF), :])
-
-    @pl.loop(0, ND)
-    def _(d):
-        pltpu.make_async_copy(
-            tok.at[:, pl.ds(0, CW)], xg.at[d, pl.ds(me * TD, TD), :], own_sem.at[d]
-        ).wait()
-        rows = pl.ds(pl.multiple_of(d * CW, CW), CW)
-
-        def part(block):
-            sga[...] += dot(block, sg[rows, :])
-            sua[...] += dot(block, su[rows, :])
-
-        first_groups(d, part)
-
-    @pl.loop(0, ND)
-    def _(d):
-        p = d + ND
-        pltpu.make_async_copy(
-            tok.at[:, pl.ds(0, CW)], xg.at[p, pl.ds(me * TD, TD), :], own_sem.at[p]
-        ).wait()
-        rows = pl.ds(pl.multiple_of(d * CW, CW), CW)
-
-        def part(block):
-            sda[...] += dot(block, sd[rows, :])
-
-        first_groups(p, part)
+                stage[k, :, here] = scaled(acc, a, k)
+            send_piece(a, cols, width, k, k)
+
+        for n in range(count):
+            block = xg[a, pl.ds(mine, HALF), units(first, n)]
+            if a == 0:
+                sga[...] += dot(block, sg[units(first, n), :])
+                sua[...] += dot(block, su[units(first, n), :])
+            else:
+                sda[...] += dot(block, sd[units(first, n), :])
+
+    first_groups(0, *PIECES[0])
+    first_groups(1, *PIECES[1])
+
+    @pl.loop(0, 2)
+    def _(j):
+        first_groups(2 + j, 0, 3 + 3 * j, 3)
+
+    @pl.loop(0, 3)
+    def _(j):
+        first_groups(4 + j, 1, 3 * j, 3)
 
     s_gate, s_up, s_hid = sga[...], sua[...], sda[...]
     sig = jax.nn.sigmoid(s_gate)
@@ -367,32 +362,30 @@
     for j, (h, v) in enumerate(weights):
         pltpu.make_async_copy(h, v, w_sem.at[j]).wait()
 
-    def late_piece(k, p):
+    def late_piece(k, a, d):
         for n in range(3):
-            cols = slice(n * 256, (n + 1) * 256)
-            acc = dot(place[rows_of(k), :], xg[p, :, cols])
-            stage[0, :, cols] = scaled(acc, p, k)
-        send_piece(p, k, 0)
+            acc = dot(place[rows_of(k), :], xg[a, :, units(3 * d, n)])
+            stage[0, :, n * UW : (n + 1) * UW] = scaled(acc, a, k)
+        send_piece(a, pl.ds(pl.multiple_of(d * CW, CW), CW), CW, k, 0)
 
     def fetch(k):
-        for d in range(ND):
-            pltpu.make_async_copy(rb.at[d, rows_of(k), :], xb.at[d], in_sem).start()
-            pltpu.make_async_copy(rb.at[ND + d, rows_of(k), :], gb.at[d], in_sem).start()
+        pltpu.make_async_copy(rb.at[0, rows_of(k), :], xb, in_sem).start()
+        pltpu.make_async_copy(rb.at[1, rows_of(k), :], gb, in_sem).start()
         wait_for(xb, in_sem)
         wait_for(gb, in_sem)
 
     def expert(k):
-        low_gate = sum(dot_last(xb[d], gin[:, d * CW : (d + 1) * CW]) for d in range(ND)).astype(BF)
-        low_up = sum(dot_last(xb[d], uin[:, d * CW : (d + 1) * CW]) for d in range(ND)).astype(BF)
+        low_gate = sum(dot_last(xb[:, d * CW : (d + 1) * CW], gin[:, d * CW : (d + 1) * CW]) for d in range(ND)).astype(BF)
+        low_up = sum(dot_last(xb[:, d * CW : (d + 1) * CW], uin[:, d * CW : (d + 1) * CW]) for d in range(ND)).astype(BF)
 
         @pl.loop(0, FF // 256)
         def _(j):
             cols = pl.ds(pl.multiple_of(j * 256, 256), 256)
-            gate = sum(dot(xb[d], gw[d * CW : (d + 1) * CW, cols]) for d in range(ND))
+            gate = sum(dot(xb[:, d * CW : (d + 1) * CW], gw[d * CW : (d + 1) * CW, cols]) for d in range(ND))
             gate = gate + dot(low_gate, gout[:, cols])
-            up = sum(dot(xb[d], uw[d * CW : (d + 1) * CW, cols]) for d in range(ND))
+            up = sum(dot(xb[:, d * CW : (d + 1) * CW], uw[d * CW : (d + 1) * CW, cols]) for d in range(ND))
             up = up + dot(low_up, uout[:, cols])
-            hid = sum(dot_last(gb[d], dw[cols, d * CW : (d + 1) * CW]) for d in range(ND))
+            hid = sum(dot_last(gb[:, d * CW : (d + 1) * CW], dw[cols, d * CW : (d + 1) * CW]) for d in range(ND))
             s = jax.nn.sigmoid(gate)
             dg[:, cols] = (hid * up * s * (1.0 + gate * (1.0 - s))).astype(BF)
             du[:, cols] = (hid * gate * s).astype(BF)
@@ -404,8 +397,8 @@
         uout_g[...] += dot_first(low_up, duv)
         for d in range(ND):
             cols = slice(d * CW, (d + 1) * CW)
-            gin_g[:, cols] += dot_first(low_dg, xb[d])
-            uin_g[:, cols] += dot_first(low_du, xb[d])
+            gin_g[:, cols] += dot_first(low_dg, xb[:, d * CW : (d + 1) * CW])
+            uin_g[:, cols] += dot_first(low_du, xb[:, d * CW : (d + 1) * CW])
 
         @pl.loop(0, ND)
         def _(d):
@@ -442,13 +435,14 @@
 
     @pl.loop(FIRST, 4)
     def _(k):
-        @pl.loop(0, NP)
+        @pl.loop(0, NA * ND)
         def _(p):
-            late_piece(k, p)
+            late_piece(k, p // ND, p % ND)
 
     hit_t = hits[...].T
+    block_row = ((lax.broadcasted_iota(jnp.int32, (TD, ROWS), 1) * 7282) >> 16) & 7
     for b in range(NB):
-        place_t[b * TD : (b + 1) * TD, :] = (hit_t * block_row[b : b + 1, :]).astype(BF)
+        place_t[b * TD : (b + 1) * TD, :] = jnp.where(block_row == b, hit_t, 0.0).astype(BF)
 
     @pl.loop(0, 4)
     def _(k):
@@ -476,7 +470,6 @@
         @pl.when(k == 3)
         def _():
             send_back(3, 4, 0, 6)
-            send_back(0, 4, 6, NU)
 
     wait_for(ret.at[:, pl.ds(0, MSG), :], r_own)
 
@@ -510,6 +503,11 @@
 
     @pl.loop(0, NU + 2)
     def _(t):
+        @pl.when((t == 1) | (t == 3) | (t == 5))
+        def _():
+            unit = jnp.clip((t + 11) // 2, 6, 8)
+            send_back(0, 4, unit, unit + 1)
+
         @pl.when(t < NU)
         def _():
             combine(jnp.minimum(t, NU - 1))
@@ -535,16 +533,6 @@
 def hand_over(*refs):
     for j in range(5):
         refs[5 + j][...] = refs[j][...].reshape(refs[5 + j].shape)
-
-
-def tables():
-    r = np.arange(ROWS)
-    i, b, s = r // MSG, (r // CAP) % NB, r % CAP
-    expand = (np.arange(TD)[None, :] == (b * NPEER + i)[:, None]).astype(np.float32)
-    slot_of = np.broadcast_to(s[:, None], (ROWS, TD)).astype(np.float32)
-    block_of = np.broadcast_to(b[:, None], (ROWS, TD)).astype(np.float32)
-    block_row = (b[None, :] == np.arange(NB)[:, None]).astype(np.float32)
-    return expand, slot_of, block_of, block_row
 
 
 def local(
@@ -563,7 +551,6 @@
     shared_up,
     shared_down,
 ):
-    expand, slot_of, block_of, block_row = tables()
     any_spec = pl.BlockSpec(memory_space=pl.ANY)
     vmem = pl.BlockSpec(memory_space=pltpu.VMEM)
     rank = gate_adapter_in.shape[1]
@@ -579,13 +566,13 @@
             shape((rank, FF), F32),
             shape((rank, D), F32),
             shape((rank, FF), F32),
-            shape((NP, ROWS, CW), BF),
-            shape((NP, ROWS, CW), BF),
+            shape((NA, ROWS, D), BF),
+            shape((NA, ROWS, D), BF),
             shape((NU, ROWS, UW), BF),
             shape((NU, ROWS, UW), BF),
         ),
         in_specs=[any_spec] * 2
-        + [vmem] * 6
+        + [vmem] * 2
         + [any_spec] * 3
         + [vmem] * 4
         + [any_spec] * 3,
@@ -599,19 +586,19 @@
             pltpu.VMEM((D, sff), BF),
             pltpu.VMEM((NB, 2, NPEER, TD), F32),
             pltpu.VMEM((NB, 2, NPEER, TD), F32),
-            pltpu.VMEM((NP, NB * TD, CW), BF),
+            pltpu.VMEM((NA, NB * TD, D), BF),
             pltpu.VMEM((ROWS, NB * TD), BF),
             pltpu.VMEM((NB * TD, ROWS), BF),
             pltpu.VMEM((ROWS, TD), F32),
             pltpu.VMEM((ROWS, TD), F32),
             pltpu.VMEM((FIRST, GR, CW), F32),
             pltpu.VMEM((FIRST, GR, CW), BF),
-            pltpu.VMEM((ND, GR, CW), BF),
-            pltpu.VMEM((ND, GR, CW), BF),
+            pltpu.VMEM((GR, D), BF),
+            pltpu.VMEM((GR, D), BF),
             pltpu.VMEM((GR, FF), BF),
             pltpu.VMEM((GR, FF), BF),
             pltpu.VMEM((NU, GR, UW), BF),
-            pltpu.VMEM((NP, MSG, CW), BF),
+            pltpu.VMEM((NA, MSG, D), BF),
             pltpu.VMEM((NU, MSG, UW), BF),
             pltpu.VMEM((HALF, sff), F32),
             pltpu.VMEM((HALF, sff), F32),
@@ -630,11 +617,11 @@
             dma,
             dma,
             dma,
-            dma((NP,)),
-            dma,
-            dma((NP, 3)),
-            dma,
-            dma((NP,)),
+            dma((len(PIECES),)),
+            dma,
+            dma((len(PIECES), 3)),
+            dma,
+            dma((len(PIECES),)),
             dma,
             dma,
             dma((4,)),
@@ -659,10 +646,6 @@
         output_grad,
         chosen_experts.T,
         route_weights.T,
-        jnp.asarray(expand, BF),
-        jnp.asarray(slot_of),
-        jnp.asarray(block_of),
-        jnp.asarray(block_row),
         gate_weight[0],
         up_weight[0],
         down_weight[0],

time: 237 us -> 223 us (0.941)
  the two profiles are of different devices: /device:TPU:16 before, /device:TPU:8 now
where the time goes in v4:
time: 223 us; the launch traced here: 222 us
  Pallas kernels  222 us (100%)
    pallas_call x1, Pallas kernels, local(): pl.pallas_call(kernel, name='moe_backward', out_shape=(shape((TD, D), BF)...  219 us

profile of v4, /device:TPU:8, one launch (start us, length us, event | category | flops | bytes accessed | tf_op | source)
XLA Modules:
  0.0 222.2 jit_solution(5518240997253142278)
XLA Ops:
  0.6 219.4 %moe_backward.1 = (bf16[128,2304]{1,0:T(8,128)(2,1)}, f32[16,2304]{1,0:T(8,128)}, f32[16,1024]{1,0:T(8,128)}, f32[16,2304]{1,0:T(8,128)}, f32[16,1024]{1,0:T(8,1...) custom-call(bf16[128,2304]{1,0:T(8,128)(2,1)} %tok.1, ...), custom_call_target="tpu_custom_call" | custom-call | tf_op jit(solution)/shard_map/moe_backward/pallas_call | solution.py:560
  220.0 2.2 hand_over.1

commit v5 on v4

--- a/solution.py
+++ b/solution.py
@@ -25,7 +25,7 @@
 HALF = 4 * TD
 UW = 256
 NU = D // UW
-FIRST = 3
+FIRST = 2
 
 
 def dot(a, b):
@@ -242,25 +242,22 @@
             remote(src, dst, gx_send, gx_recv.at[p, o - 1], x_peer(o)).start()
         remote(src, dst, gc_send, gc_recv.at[p], sibling()).start()
 
-    row = lax.broadcasted_iota(jnp.int32, (ROWS, TD), 0)
-    lane = lax.broadcasted_iota(jnp.int32, (ROWS, TD), 1)
-    nine = (row * 7282) >> 16
-    slot_of = (row - CAP * nine).astype(F32)
-    block_of = nine & 7
-    spread = jnp.where(lane == block_of * NPEER + (nine >> 3), 1.0, 0.0).astype(BF)
+    def message_rows():
+        row = lax.broadcasted_iota(jnp.int32, (ROWS, TD), 0)
+        lane = lax.broadcasted_iota(jnp.int32, (ROWS, TD), 1)
+        nine = (row * 7282) >> 16
+        slot = (row - CAP * nine).astype(F32)
+        block = nine & 7
+        spread = jnp.where(lane == block * NPEER + (nine >> 3), 1.0, 0.0).astype(BF)
+        return spread, block, slot
+
+    spread, block_of, slot_of = message_rows()
 
     own_meta.wait()
     wait_for(meta_all.at[pl.ds(0, 7)], m_recv)
 
     code = meta_all[:, 0].reshape(TD, TD).astype(BF)
     hit = jnp.where(dot(spread, code) == slot_of, 1.0, 0.0)
-    w_all = meta_all[:, 1].reshape(TD, TD)
-    w_hi = w_all.astype(BF)
-    left = w_all - w_hi.astype(F32)
-    w_mid = left.astype(BF)
-    w_lo = (left - w_mid.astype(F32)).astype(BF)
-    w_row = (dot(spread, w_hi) + dot(spread, w_mid)) + dot(spread, w_lo)
-    wsl[...] = jnp.broadcast_to(jnp.sum(w_row * hit, axis=1, keepdims=True), (ROWS, TD))
     hits[...] = hit
     for b in range(NB):
         place[:, b * TD : (b + 1) * TD] = jnp.where(block_of == b, hit, 0.0).astype(BF)
@@ -298,6 +295,8 @@
                 pltpu.make_async_copy(kept.at[a, :, cols], rb.at[a, rows, cols], d_own).start()
 
     def scaled(acc, a, k):
+        if isinstance(a, int) and a == 0:
+            return acc.astype(BF)
         scale = jnp.where(a == 0, 1.0, wsl[rows_of(k), :][:, 0:1])
         return (acc * scale).astype(BF)
 
@@ -349,6 +348,15 @@
     @pl.loop(0, 2)
     def _(j):
         first_groups(2 + j, 0, 3 + 3 * j, 3)
+
+    again = message_rows()[0]
+    w_all = meta_all[:, 1].reshape(TD, TD)
+    w_hi = w_all.astype(BF)
+    left = w_all - w_hi.astype(F32)
+    w_mid = left.astype(BF)
+    w_lo = (left - w_mid.astype(F32)).astype(BF)
+    w_row = (dot(again, w_hi) + dot(again, w_mid)) + dot(again, w_lo)
+    wsl[...] = jnp.broadcast_to(jnp.sum(w_row * hits[...], axis=1, keepdims=True), (ROWS, TD))
 
     @pl.loop(0, 3)
     def _(j):

time: 223 us -> 219 us (0.982)
  Pallas kernels: 222 us -> 218 us
    pallas_call x1, Pallas kernels: 219 us -> 216 us  [local(): pl.pallas_call(kernel, name='moe_backward', out_shape=(shape((TD, D), BF)...]
where the time goes in v5:
time: 219 us
  Pallas kernels  218 us (100%)
    pallas_call x1, Pallas kernels, local(): pl.pallas_call(kernel, name='moe_backward', out_shape=(shape((TD, D), BF)...  216 us

profile of v5, /device:TPU:8, one launch (start us, length us, event | category | flops | bytes accessed | tf_op | source)
XLA Modules:
  0.0 218.6 jit_solution(197154634487214074)
XLA Ops:
  0.6 215.8 %moe_backward.1 = (bf16[128,2304]{1,0:T(8,128)(2,1)}, f32[16,2304]{1,0:T(8,128)}, f32[16,1024]{1,0:T(8,128)}, f32[16,2304]{1,0:T(8,128)}, f32[16,1024]{1,0:T(8,1...) custom-call(bf16[128,2304]{1,0:T(8,128)(2,1)} %tok.1, ...), custom_call_target="tpu_custom_call" | custom-call | tf_op jit(solution)/shard_map/moe_backward/pallas_call | solution.py:568
  216.4 2.2 hand_over.1

commit v6 on v5

--- a/solution.py
+++ b/solution.py
@@ -473,11 +473,12 @@
 
         @pl.when(k == 2)
         def _():
-            send_back(0, 3, 3, 6)
+            send_back(0, 3, 3, 5)
 
         @pl.when(k == 3)
         def _():
-            send_back(3, 4, 0, 6)
+            send_back(3, 4, 0, 5)
+            send_back(0, 4, 5, 6)
 
     wait_for(ret.at[:, pl.ds(0, MSG), :], r_own)
 

time: 219 us -> 215 us (0.982)
  Pallas kernels: 218 us -> 213 us
    pallas_call x1, Pallas kernels: 216 us -> 211 us  [local(): pl.pallas_call(kernel, name='moe_backward', out_shape=(shape((TD, D), BF)...]
where the time goes in v6:
time: 215 us; the launch traced here: 214 us
  Pallas kernels  213 us (99%)
    pallas_call x1, Pallas kernels, local(): pl.pallas_call(kernel, name='moe_backward', out_shape=(shape((TD, D), BF)...  211 us

profile of v6, /device:TPU:8, one launch (start us, length us, event | category | flops | bytes accessed | tf_op | source)
XLA Modules:
  0.0 214.1 jit_solution(6235191870821202081)
XLA Ops:
  0.6 211.3 %moe_backward.1 = (bf16[128,2304]{1,0:T(8,128)(2,1)}, f32[16,2304]{1,0:T(8,128)}, f32[16,1024]{1,0:T(8,128)}, f32[16,2304]{1,0:T(8,128)}, f32[16,1024]{1,0:T(8,1...) custom-call(bf16[128,2304]{1,0:T(8,128)(2,1)} %tok.1, ...), custom_call_target="tpu_custom_call" | custom-call | tf_op jit(solution)/shard_map/moe_backward/pallas_call | solution.py:569
  211.9 2.2 %hand_over.1 = (bf16[128,2304]{1,0:T(8,128)(2,1)}, f32[1,16,2304]{2,1,0:T(8,128)}, f32[1,16,1024]{2,1,0:T(8,128)}, f32[1,16,2304]{2,1,0:T(8,128)}, f32[1,16,1024]{2,1,0:T(8,128)}) custom-call(bf16[128,2304]{1,0:T(8,128)(2,1)} %get-tuple-element.10.refs_0_, f32[16,2304]{1,0:T(8,128)} %get-tuple-element.11.refs_1_, f32[16,1024]{1,0:T(8,128)} %get-tuple-element.12.refs_2_, ...), custom_call_target="tpu_custom_call" | custom-call | tf_op jit(solution)/shard_map/hand_over/pallas_call | solution.py:669
